TPU v7x, 256 devices: a whole 4x4x8 slice. The times are simulated.
256 devices in a mesh: row: 4 (over y_lo, core), col: 64 (over y_hi, z, x).
Axes of the slice: x: 4, y: 4 (y_hi: 2, y_lo: 2; y = y_hi * 2 + y_lo), z: 8, core: 2. Of those that a mesh axis runs over, the one named last changes fastest.
Arguments:
- matrix: float32 [8192, 32768], P('row', 'col')
- pivots: int32 [256], replicated, may hold values from 0 to 8191, as said below
- l_inverse: float32 [256, 256], replicated, as said below
Outputs:
- updated: float32 [8192, 32768], P('row', 'col')
- u_block: float32 [256, 32768], P(None, 'col')
- moved: float32 [1024, 32768], P('row', 'col')
Inputs may be any that keep to these rules, and one draw needn't show every extreme that they name: Each pivots[i] is either i or a global row number of 256 or more; pivots[0] is 0; all entries are distinct. `l_inverse`: unit lower triangular.
All inputs are finite; a program needn't handle non-finite values.
Results may differ from a plain program's by a relative error of at most 0.00058.
Values may be sent and summed in bfloat16 or wider, within the bound.
A program may use at most 64 MiB of HBM per device.

v0:
```python
import jax
import jax.numpy as jnp
from jax import lax
from jax.sharding import PartitionSpec as P


def spread(x, axis, root):
    mine = lax.axis_index(axis) == root
    return lax.psum(jnp.where(mine, x, jnp.zeros_like(x)), axis)


def body(matrix, pivots, l_inverse):
    rows_here, cols_here = matrix.shape
    width = l_inverse.shape[0]
    row_count = lax.axis_size("row")
    my_row = lax.axis_index("row")
    my_col = lax.axis_index("col")
    block = pivots // width
    owner = block % row_count
    local = block // row_count * width + pivots % width
    mine = owner == my_row
    picked = jnp.where(mine[:, None], matrix[jnp.where(mine, local, 0)], 0.0)
    top_rows = jnp.where(my_row == 0, matrix[:width], 0.0)
    picked, top_rows = lax.psum((picked, top_rows), "row")
    target = jnp.where(mine, local, rows_here)
    swapped = matrix.at[target].set(top_rows, mode="drop")
    u_rows = jnp.dot(
        l_inverse, picked, precision=lax.Precision.HIGHEST, preferred_element_type=jnp.float32
    )
    u_half = u_rows.astype(jnp.bfloat16)
    l_panel = matrix[:, :width].astype(jnp.bfloat16)
    whole = spread(l_panel, "col", 0)
    update = jnp.dot(whole, u_half, preferred_element_type=jnp.float32)
    result = swapped - update
    head = jnp.where(my_row == 0, u_rows, result[:width])
    result = result.at[:width].set(head)
    column = jnp.arange(cols_here)
    is_panel = (my_col == 0) & (column < width)
    final = jnp.where(is_panel[None, :], matrix, result)
    landed = mine & (pivots >= width)
    moved = jnp.where(landed[:, None], final[jnp.where(landed, local, 0)], 0.0)
    return (final, u_rows, moved)


def solution(mesh):
    return jax.shard_map(
        body,
        mesh=mesh,
        in_specs=(P("row", "col"), P(), P()),
        out_specs=(P("row", "col"), P(None, "col"), P("row", "col")),
        check_vma=False,
    )
```

profile of v0, /device:TPU:2, one launch (start us, length us, event | category | flops | bytes accessed | tf_op | source)
XLA Modules:
  0.0 793.4 jit_solution(5658228010464229565)
XLA Ops:
  7.2 0.0 copy-start
  7.2 0.0 copy-start.3
  7.2 0.0 all-reduce.6.cloned.1.call-start
  7.2 4.7 copy.24
  11.9 0.0 copy-done.3
  12.0 5.4 copy.11
  17.4 3.4 gather_fusion
  20.8 0.2 copy.8
  21.0 0.8 broadcast_select_fusion.2
  21.8 1.9 slice_select_fusion.1
  23.7 0.0 all-reduce.6.cloned.1.call-update
  23.7 0.0 all-reduce.4.cloned.1.call-start
  23.7 2.7 fusion
  26.4 0.0 all-reduce.4.cloned.1.call-update
  26.5 47.1 %all-reduce.6.cloned.1.call-done = (f32[256,512]{0,1:T(8,128)}, f32[256,512]{0,1:T(8,128)}) async-done(((f32[256,512]{0,1:T(8,128)}, f32[256,512]{0,1:T(8,128)}), (f32[256,512]{0,1:T(8,128)}, f32[256,512]{0,1:T(8,128)})) %all-reduce.6.cloned.1.call-update) | async-done | bytes 1048592 | tf_op jit(solution)/shard_map/psum | solution.py:24
  73.6 1.2 copy.7
  74.8 5.6 scatter_fusion
  80.4 0.0 copy-start.2
  80.4 5.5 copy.9
  85.9 0.0 copy-done
  85.9 0.0 copy-done.2
  85.9 0.6 convolution_bitcast_fusion
  86.5 1.0 copy.15
  87.5 682.9 %all-reduce.4.cloned.1.call-done = bf16[2048,256]{1,0:T(8,128)(2,1)} async-done(((bf16[2048,256]{1,0:T(8,128)(2,1)}), bf16[2048,256]{1,0:T(8,128)(2,1)}) %all-reduce.4.cloned.1.call-update) | async-done | bytes 1048592 | tf_op jit(solution)/shard_map/psum | solution.py:9
  770.4 0.0 copy-start.1
  770.4 3.4 convolution_subtract_fusion
  773.8 0.1 fusion.1
  773.9 0.2 copy-done.1
  774.1 2.4 broadcast_select_fusion
  776.6 5.3 copy.14
  781.9 3.4 gather_fusion.1
  785.3 0.2 copy.13
  785.5 1.0 copy.16
  (6 shorter events, 0.1 us)
Async XLA Ops:
  7.2 78.7 %copy-start = (f32[256,256]{1,0:T(8,128)S(1)}, f32[256,256]{1,0:T(8,128)}, u32[]{:S(2)}) copy-start(f32[256,256]{1,0:T(8,128)} %param.7) | copy-start | bytes 786436
  7.2 4.7 copy-start.3
  7.2 66.4 %all-reduce.6.cloned.1.call-start = ((), (), s32[]{:S(2)}) async-start(), calls=%async_computation.1 | async-start | bytes 2097152 | tf_op jit(solution)/shard_map/psum | solution.py:24
  23.7 746.7 %all-reduce.4.cloned.1.call-start = ((), (), s32[]{:S(2)}) async-start(), calls=%async_computation | async-start | bytes 2097152 | tf_op jit(solution)/shard_map/psum | solution.py:9
  80.4 5.5 copy-start.2
  770.4 3.7 copy-start.1
Sparse Core Ops, SparseCore 0:
  23.8 49.7 all-reduce.5
  76.4 693.9 all-reduce.3
where the time goes:
time: 794 us; the launch traced here: 793 us
  waiting for transfers between devices  730 us (92%)
  local copies, waits for them, and re-layouts  37.1 us (5%)
  between operations  14.2 us (2%)
  other arithmetic  7.99 us (1%)
    psum x1, waiting for transfers between devices, spread(): return lax.psum(jnp.where(mine, x, jnp.zeros_like(x)), axis)  683 us
    psum x1, waiting for transfers between devices, body(): picked, top_rows = lax.psum((picked, top_rows), 'row')  47.1 us
    unnamed x13, local copies, waits for them, and re-layouts  17.6 us
  transfers between devices with their start and end apart: 2, of which 2 were waited for; matrix products, arithmetic and copies ran while one was open for 2% of the time, Pallas kernels for 0%

commit v1 on v0

v1 whole, which is shorter than its diff:
```python
import functools

import jax
import jax.numpy as jnp
from jax import lax
from jax.experimental import pallas as pl
from jax.experimental.pallas import tpu as pltpu
from jax.sharding import PartitionSpec as P

CHUNKS = 16
TILES = 8
SLOTS = 4
NZ = 8
NX = 4


def pick(cond, a, b):
    return jnp.where(cond, a, b)


def column(yh, z, x):
    return (yh * NZ + z) * NX + x


def tree(core, yh, z, x):
    first = core == 0
    root = (yh == 0) & (x == 0)
    flat = z == 0
    up = (z >= 1) & (z <= 3)
    down = (z == 6) | (z == 7)
    step = pick(up, z + 1, z - 1)
    a0 = pick(first, jnp.logical_not(root), root)
    v0 = (flat | up | down) & a0
    k0 = column(yh, pick(flat, 1, step), x)
    inplane = pick(first, flat, jnp.logical_not(flat))
    zlow = flat & a0
    s1x = inplane & (x <= 1)
    v1 = s1x
    k1 = column(yh, z, x + 1)
    wrap = inplane & (x == 0)
    back = first & (yh == 0) & (x == 1) & jnp.logical_not(flat)
    drop = jnp.logical_not(first) & (z == 1) & jnp.logical_not(root)
    v2 = wrap | back
    k2 = column(yh, z, pick(wrap, 3, 0))
    cross = inplane & root
    v3 = cross | zlow | drop
    k3 = pick(cross, column(1, z, x), column(yh, pick(drop, 0, 7), x))
    kids = ((v0, k0), (v1, k1), (v2, k2), (v3, k3))
    zback = pick(z <= 4, z - 1, (z + 1) % NZ)
    px = pick(x == 2, 1, 0)
    inparent = pick(x == 0, column(0, z, 0), column(yh, z, px))
    p_first = pick(
        flat, inparent, pick(root, column(0, z, 1), column(yh, zback, x))
    )
    p_second = pick(
        root, column(0, zback, 0), pick(flat, column(yh, 1, x), inparent)
    )
    return kids, pick(first, p_first, p_second)


def move_kernel(
    idx, mask, mat_hbm, panel, w_me, w_pair, m_far, mat, comb,
    in_sem, recv_sem, send_sem, x_send, x_recv,
):
    r = lax.axis_index("row")
    c = lax.axis_index("col")
    core = r % 2
    yl = r // 2
    x = c % NX
    z = (c // NX) % NZ
    yh = c // (NX * NZ)
    pair = yl * 2 + 1 - core
    far = (1 - yl) * 2 + core
    source = c == 0
    kids, parent = tree(core, yh, z, x)
    rows = mat_hbm.shape[0]
    tile = rows // TILES
    chunk = rows // CHUNKS
    per = CHUNKS // TILES
    width = panel.shape[1]
    nb = w_me.shape[0]

    def load(t):
        at = pl.ds(pl.multiple_of(t * tile, tile), tile)
        return pltpu.make_async_copy(mat_hbm.at[at], mat.at[at], in_sem.at[t])

    def forward(j, k):
        at = pl.ds(pl.multiple_of(j * chunk, chunk), chunk)
        return pltpu.make_async_remote_copy(
            src_ref=panel.at[at],
            dst_ref=panel.at[at],
            send_sem=send_sem.at[k],
            recv_sem=recv_sem.at[j],
            device_id={"row": r, "col": kids[k][1]},
            device_id_type=pl.DeviceIdType.MESH,
        )

    def send(j):
        for k in range(SLOTS):
            @pl.when(kids[k][0])
            def _():
                forward(j, k).start()

    for t in range(TILES):
        load(t).start()

    barrier = pltpu.get_barrier_semaphore()

    @pl.when(jnp.logical_not(source))
    def _():
        pl.semaphore_signal(
            barrier, inc=1, device_id={"row": r, "col": parent}, device_id_type=pl.DeviceIdType.MESH
        )

    for other in (pair, far):
        pl.semaphore_signal(
            barrier, inc=1, device_id={"row": other, "col": c}, device_id_type=pl.DeviceIdType.MESH
        )
    expect = 2
    for k in range(SLOTS):
        expect = expect + kids[k][0].astype(jnp.int32)
    pl.semaphore_wait(barrier, expect)

    @pl.when(source)
    def _():
        @pl.loop(0, TILES)
        def _(t):
            load(t).wait()
            at = pl.ds(pl.multiple_of(t * tile, tile), tile)
            panel[at] = mat[at, :width].astype(panel.dtype)
            for s in range(per):
                send(t * per + s)

    @pl.when(jnp.logical_not(source))
    def _():
        @pl.loop(0, TILES)
        def _(t):
            load(t).wait()

    @pl.loop(0, nb // 8)
    def _(g):
        for s in range(8):
            i = g * 8 + s
            w_me[pl.ds(i, 1)] = mat[pl.ds(idx[i], 1)]

    swap = pltpu.make_async_remote_copy(
        src_ref=w_me, dst_ref=w_pair, send_sem=x_send.at[0], recv_sem=x_recv.at[0],
        device_id={"row": pair, "col": c}, device_id_type=pl.DeviceIdType.MESH,
    )
    swap.start()
    swap.wait()
    comb[...] = jnp.where(mask[...] == 1, w_pair[...], w_me[...])
    across = pltpu.make_async_remote_copy(
        src_ref=comb, dst_ref=m_far, send_sem=x_send.at[1], recv_sem=x_recv.at[1],
        device_id={"row": far, "col": c}, device_id_type=pl.DeviceIdType.MESH,
    )
    across.start()

    @pl.when(jnp.logical_not(source))
    def _():
        @pl.loop(0, CHUNKS)
        def _(j):
            forward(j, 0).wait_recv()
            send(j)

    across.wait()
    whole = pltpu.make_async_remote_copy
    for k in range(SLOTS):
        @pl.when(kids[k][0])
        def _():
            whole(
                src_ref=panel, dst_ref=panel, send_sem=send_sem.at[k], recv_sem=recv_sem.at[0],
                device_id={"row": r, "col": kids[k][1]}, device_id_type=pl.DeviceIdType.MESH,
            ).wait_send()


def finish_kernel(
    dst, src, flags, mat_hbm, panel, w_me, w_pair, m_far, code, l_inverse,
    out_hbm, u_ref, moved, mat, u_half, top, in_sem, out_sem,
):
    rows = out_hbm.shape[0]
    tile = rows // TILES
    nb = u_ref.shape[0]
    width = panel.shape[1]
    me = flags[0]
    owns_panel = flags[1] == 1

    def piece(t):
        return pl.ds(pl.multiple_of(t * tile, tile), tile)

    def load(t):
        return pltpu.make_async_copy(mat_hbm.at[piece(t)], mat.at[piece(t)], in_sem.at[t])

    def store(t):
        return pltpu.make_async_copy(mat.at[piece(t)], out_hbm.at[piece(t)], out_sem.at[t])

    for t in range(TILES):
        load(t).start()
    who = code[...]
    picked = jnp.where(who == 0, w_me[...], jnp.where(who == 1, w_pair[...], m_far[...]))
    u = jnp.dot(
        l_inverse[...], picked, precision=lax.Precision.HIGHEST, preferred_element_type=jnp.float32
    )
    u_ref[...] = u
    u_half[...] = u.astype(u_half.dtype)

    for t in range(TILES):
        load(t).wait()

    @pl.when(me == 0)
    def _():
        top[...] = mat[pl.ds(0, nb)]

    @pl.when(me == 1)
    def _():
        top[...] = w_pair[...]

    @pl.when(me >= 2)
    def _():
        top[...] = m_far[...]

    @pl.when(owns_panel)
    def _():
        top[:, :width] = w_me[:, :width]

    mat[pl.ds(rows + 8, 8)] = jnp.zeros((8, mat.shape[1]), mat.dtype)

    @pl.loop(0, nb // 8)
    def _(g):
        for s in range(8):
            i = g * 8 + s
            mat[pl.ds(dst[i], 1)] = top[pl.ds(i, 1)]

    @pl.loop(0, TILES)
    def _(t):
        at = piece(t)
        old = mat[at]
        new = old - jnp.dot(panel[at], u_half[...], preferred_element_type=jnp.float32)
        new = jnp.where((t == 0) & (me == 0), u_ref[...], new)
        mat[at, :width] = jnp.where(owns_panel, old[:, :width], new[:, :width])
        mat[at, width:] = new[:, width:]
        store(t).start()

    @pl.loop(0, nb // 8)
    def _(g):
        for s in range(8):
            i = g * 8 + s
            moved[pl.ds(i, 1)] = mat[pl.ds(src[i], 1)]

    for t in range(TILES):
        store(t).wait()


def body(matrix, pivots, l_inverse):
    rows, cols = matrix.shape
    nb = l_inverse.shape[0]
    f32, bf16 = jnp.float32, jnp.bfloat16
    row_count = lax.axis_size("row")
    me = lax.axis_index("row")
    my_col = lax.axis_index("col")
    block = pivots // nb
    owner = block % row_count
    local = block // row_count * nb + pivots % nb
    mine = owner == me
    landed = mine & (pivots >= nb)
    pair = me + 1 - 2 * (me % 2)
    idx = jnp.where(mine, local, jnp.arange(nb)).astype(jnp.int32)
    from_pair = jnp.where(me % 2 == 1, owner != me, owner == pair)
    mask = from_pair.astype(jnp.int32)[:, None]
    code = jnp.where(mine, 0, jnp.where(owner == pair, 1, 2)).astype(jnp.int32)[:, None]
    dst = jnp.where(landed, local, rows).astype(jnp.int32)
    src = jnp.where(landed, local, rows + 8).astype(jnp.int32)
    flags = jnp.stack([me, my_col == 0]).astype(jnp.int32)
    vmem = pl.BlockSpec(memory_space=pltpu.VMEM)
    smem = pl.BlockSpec(memory_space=pltpu.SMEM)
    hbm = pl.BlockSpec(memory_space=pl.ANY)
    shape = jax.ShapeDtypeStruct
    panel, w_me, w_pair, m_far = pl.pallas_call(
        move_kernel,
        out_shape=(
            shape((rows, nb), bf16), shape((nb, cols), f32),
            shape((nb, cols), f32), shape((nb, cols), f32),
        ),
        in_specs=[smem, vmem, hbm],
        out_specs=[vmem] * 4,
        scratch_shapes=[
            pltpu.VMEM((rows, cols), f32),
            pltpu.VMEM((nb, cols), f32),
            pltpu.SemaphoreType.DMA((TILES,)),
            pltpu.SemaphoreType.DMA((CHUNKS,)),
            pltpu.SemaphoreType.DMA((SLOTS,)),
            pltpu.SemaphoreType.DMA((2,)),
            pltpu.SemaphoreType.DMA((2,)),
        ],
        compiler_params=pltpu.CompilerParams(collective_id=0, has_side_effects=True),
        name="move",
    )(idx, mask, matrix)
    return pl.pallas_call(
        finish_kernel,
        out_shape=(shape((rows, cols), f32), shape((nb, cols), f32), shape((nb, cols), f32)),
        in_specs=[smem, smem, smem, hbm] + [vmem] * 6,
        out_specs=[hbm, vmem, vmem],
        scratch_shapes=[
            pltpu.VMEM((rows + 16, cols), f32),
            pltpu.VMEM((nb, cols), bf16),
            pltpu.VMEM((nb, cols), f32),
            pltpu.SemaphoreType.DMA((TILES,)),
            pltpu.SemaphoreType.DMA((TILES,)),
        ],
        name="finish",
    )(dst, src, flags, matrix, panel, w_me, w_pair, m_far, code, l_inverse)


def solution(mesh):
    return jax.shard_map(
        body,
        mesh=mesh,
        in_specs=(P("row", "col"), P(), P()),
        out_specs=(P("row", "col"), P(None, "col"), P("row", "col")),
        check_vma=False,
    )
```

time: 794 us -> 55.6 us (0.07)
  the two profiles are of different devices: /device:TPU:2 before, /device:TPU:156 now
where the time goes in v1:
time: 55.6 us; the launch traced here: 55.4 us
  Pallas kernels  48.9 us (88%)
  other arithmetic  4.31 us (8%)
  local copies, waits for them, and re-layouts  1.59 us (3%)
  between operations  0.67 us (1%)
    pallas_call x1, Pallas kernels, body(): pl.pallas_call(move_kernel, out_shape=(shape((rows, nb), bf16), shape((nb...  40.1 us
    pallas_call x1, Pallas kernels, body(): pl.pallas_call(finish_kernel, out_shape=(shape((rows, cols), f32), shape(...  8.78 us
    select_n x1, other arithmetic, body(): src = jnp.where(landed, local, rows + 8).astype(jnp.int32)  1.26 us
    select_n x1, other arithmetic, body(): idx = jnp.where(mine, local, jnp.arange(nb)).astype(jnp.int32)  1.25 us

profile of v1, /device:TPU:156, one launch (start us, length us, event | category | flops | bytes accessed | tf_op | source)
XLA Modules:
  0.0 55.4 jit_solution(4814252106878454421)
XLA Ops:
  0.7 0.6 pad_add_fusion.flags
  1.2 0.7 %select_select_fusion = (s32[256]{0:T(256)S(1)}, s32[256]{0:T(256)S(1)}, s32[256]{0:T(256)S(1)}) fusion(s32[]{:T(128)S(6)} %sub.15, s32[]{:T(128)} %axis_index.23, s32[256]{0:T(256)} %param.4), kind=kLoop, calls=%fused_computation.13 | loop fusion | flops 7680 | bytes 4104 | tf_op jit(solution)/shard_map/jit(_where)/select_n | solution.py:270
  1.9 1.3 %iota_select_fusion = (s32[256]{0:T(256)}, s32[256]{0:T(256)S(1)}) fusion(s32[256]{0:T(256)S(1)} %get-tuple-element.12, s32[]{:T(128)} %axis_index.23, s32[256]{0:T(256)} %param.4, s32[256]{0:T(256)S(1)} %get-tuple-element.13), kind=kLoop, calls=%fused_computation.14 | loop fusion | flops 7680 | bytes 5124 | tf_op jit(solution)/shard_map/jit(_where)/select_n | solution.py:267
  3.2 1.3 %broadcast_select_fusion = (s32[256]{0:T(256)}, pred[256]{0:T(512)(128)(4,1)S(1)}) fusion(s32[256]{0:T(256)S(1)} %get-tuple-element.15, s32[256]{0:T(256)} %param.4, s32[256]{0:T(256)S(1)} %get-tuple-element.12, s32[]{:T(128)} %axis_index.23), kind=kLoop, calls=%fused_computation.17 | loop fusion | flops 1024 | bytes 4356 | tf_op jit(solution)/shard_map/jit(_where)/select_n | solution.py:272
  4.4 0.5 broadcast_select_fusion.1.dst
  5.0 0.8 %copy.7.code = s32[256,1]{1,0:T(8,128)} copy(s32[256,1]{0,1:T(1,128)S(1)} %bitcast.5) | data formatting | bytes 2048 | tf_op jit(solution)/shard_map/broadcast_in_dim | solution.py:270
  5.8 0.8 %copy.6.mask = s32[256,1]{1,0:T(8,128)} copy(s32[256,1]{0,1:T(1,128)S(1)} %bitcast.4) | data formatting | bytes 2048 | tf_op jit(solution)/shard_map/broadcast_in_dim | solution.py:269
  6.6 40.1 %move.1 = (bf16[2048,256]{1,0:T(8,128)(2,1)}, f32[256,512]{1,0:T(8,128)}, f32[256,512]{1,0:T(8,128)}, f32[256,512]{1,0:T(8,128)}) custom-call(s32[256]{0:T(256)} %get-tuple-element.14.idx, s32[256,1]{1,0:T(8,128)} %copy.6.mask, f32[2048,512]{1,0:T(8,128)} %mat_hbm.3), custom_call_target="tpu_custom_call" | custom-call | tf_op jit(solution)/shard_map/move/pallas_call | solution.py:278
  46.7 8.8 %finish.1 = (f32[2048,512]{1,0:T(8,128)}, f32[256,512]{1,0:T(8,128)}, f32[256,512]{1,0:T(8,128)}) custom-call(s32[256]{0:T(256)} %broadcast_select_fusion.1.dst, s32[256]{0:T(256)} %get-tuple-element.16.src, s32[2]{0:T(128)} %pad_add_fusion.flags, f32[2048,512]{1,0:T(8,128)} %mat_hbm.3, bf16[2048,256]{1,0:T(8,128)(2,1)} %get-tuple-element.7.panel, ...), custom_call_target="tpu_custom_call" | custom-call | tf_op jit(solution)/shard_map/finish/pallas_call | solution.py:298
  (1 shorter events, 0.0 us)

commit v2 on v1

v2 whole, which is shorter than its diff:
```python
import jax
import jax.numpy as jnp
from jax import lax
from jax.experimental import pallas as pl
from jax.experimental.pallas import tpu as pltpu
from jax.sharding import PartitionSpec as P

CHUNKS = 32
TILES = 8
SLOTS = 4
MOVE_VMEM = 20 * 2**20
FINISH_VMEM = 20 * 2**20
NZ = 8
NX = 4


def pick(cond, a, b):
    return jnp.where(cond, a, b)


def column(yh, z, x):
    return (yh * NZ + z) * NX + x


def tree(core, yh, z, x):
    first = core == 0
    root = (yh == 0) & (x == 0)
    flat = z == 0
    up = (z >= 1) & (z <= 3)
    down = (z == 6) | (z == 7)
    step = pick(up, z + 1, z - 1)
    a0 = pick(first, jnp.logical_not(root), root)
    v0 = (flat | up | down) & a0
    k0 = column(yh, pick(flat, 1, step), x)
    inplane = pick(first, flat, jnp.logical_not(flat))
    zlow = flat & a0
    s1x = inplane & (x <= 1)
    v1 = s1x
    k1 = column(yh, z, x + 1)
    wrap = inplane & (x == 0)
    back = first & (yh == 0) & (x == 1) & jnp.logical_not(flat)
    drop = jnp.logical_not(first) & (z == 1) & jnp.logical_not(root)
    v2 = wrap | back
    k2 = column(yh, z, pick(wrap, 3, 0))
    cross = inplane & root
    v3 = cross | zlow | drop
    k3 = pick(cross, column(1, z, x), column(yh, pick(drop, 0, 7), x))
    kids = ((v0, k0), (v1, k1), (v2, k2), (v3, k3))
    zback = pick(z <= 4, z - 1, (z + 1) % NZ)
    px = pick(x == 2, 1, 0)
    inparent = pick(x == 0, column(0, z, 0), column(yh, z, px))
    p_first = pick(
        flat, inparent, pick(root, column(0, z, 1), column(yh, zback, x))
    )
    p_second = pick(
        root, column(0, zback, 0), pick(flat, column(yh, 1, x), inparent)
    )
    return kids, pick(first, p_first, p_second)


def grid_place():
    r = lax.axis_index("row")
    c = lax.axis_index("col")
    return r, c, r % 2, r // 2, c // (NX * NZ), (c // NX) % NZ, c % NX


def hops(core, yh, z, x):
    dz = jnp.minimum(z, NZ - z)
    dx = jnp.minimum(x, NX - x)
    return dz + dx + yh


def local_row(p, nb, row_count):
    shift = nb.bit_length() - 1
    deal = row_count.bit_length() - 1
    block = jnp.right_shift(p, shift)
    owner = block & (row_count - 1)
    local = jnp.left_shift(jnp.right_shift(block, deal), shift) + (p & (nb - 1))
    return owner, local


def move_kernel(
    pivots, pivot_row, mat_hbm, l_hbm, panel, mat, u_ref, top,
    w_me, w_pair, m_far, comb, code, l_inverse,
    in_sem, recv_sem, send_sem, x_send, x_recv,
):
    r, c, core, yl, yh, z, x = grid_place()
    pair = yl * 2 + 1 - core
    far = (1 - yl) * 2 + core
    source = c == 0
    kids, parent = tree(core, yh, z, x)
    rows, cols = mat_hbm.shape
    tile = rows // TILES
    chunk = rows // CHUNKS
    per = CHUNKS // TILES
    width = panel.shape[1]
    nb = w_me.shape[0]
    half = nb // 2
    row_count = lax.axis_size("row")

    def load(t):
        at = pl.ds(pl.multiple_of(t * tile, tile), tile)
        return pltpu.make_async_copy(mat_hbm.at[at], mat.at[at], in_sem.at[t])

    def forward(j, k):
        at = pl.ds(pl.multiple_of(j * chunk, chunk), chunk)
        return pltpu.make_async_remote_copy(
            src_ref=panel.at[at],
            dst_ref=panel.at[at],
            send_sem=send_sem.at[k],
            recv_sem=recv_sem.at[j],
            device_id={"row": r, "col": kids[k][1]},
            device_id_type=pl.DeviceIdType.MESH,
        )

    def send(j):
        for k in range(SLOTS):
            @pl.when(kids[k][0])
            def _():
                forward(j, k).start()

    def swap(step, src, dst, other):
        return pltpu.make_async_remote_copy(
            src_ref=src, dst_ref=dst, send_sem=x_send.at[step], recv_sem=x_recv.at[step],
            device_id={"row": other, "col": c}, device_id_type=pl.DeviceIdType.MESH,
        )

    mine = pl.ds(pl.multiple_of(core * half, half), half)
    with_pair = swap(0, w_me, w_pair, pair)
    across = swap(1, comb, m_far.at[mine], far)
    pass_on = swap(2, m_far.at[mine], m_far.at[mine], pair)

    for t in range(TILES):
        load(t).start()
    load_l = pltpu.make_async_copy(l_hbm, l_inverse, in_sem.at[TILES])
    load_l.start()

    barrier = pltpu.get_barrier_semaphore()

    @pl.when(jnp.logical_not(source))
    def _():
        pl.semaphore_signal(
            barrier, inc=1, device_id={"row": r, "col": parent}, device_id_type=pl.DeviceIdType.MESH
        )

    for other in (pair, far):
        pl.semaphore_signal(
            barrier, inc=1, device_id={"row": other, "col": c}, device_id_type=pl.DeviceIdType.MESH
        )

    owner, _ = local_row(pivot_row[...], nb, row_count)
    kind = jnp.where(owner == r, 0.0, jnp.where(owner == pair, 1.0, 2.0))
    down = lax.broadcasted_iota(jnp.int32, (nb, nb), 0)
    along = lax.broadcasted_iota(jnp.int32, (nb, nb), 1)
    spread = jnp.where(down == along, jnp.broadcast_to(kind, (nb, nb)), 0.0)
    code[...] = jnp.sum(spread, axis=1, keepdims=True)

    expect = 2
    for k in range(SLOTS):
        expect = expect + kids[k][0].astype(jnp.int32)
    pl.semaphore_wait(barrier, expect)

    @pl.when(source)
    def _():
        @pl.loop(0, TILES)
        def _(t):
            load(t).wait()
            at = pl.ds(pl.multiple_of(t * tile, tile), tile)
            panel[at] = mat[at, :width].astype(panel.dtype)
            for s in range(per):
                send(t * per + s)

    @pl.when(jnp.logical_not(source))
    def _():
        @pl.loop(0, TILES)
        def _(t):
            load(t).wait()

    @pl.loop(0, nb // 8)
    def _(g):
        for s in range(8):
            i = g * 8 + s
            own, local = local_row(pivots[i], nb, row_count)
            w_me[pl.ds(i, 1)] = mat[pl.ds(jnp.where(own == r, local, i), 1)]

    with_pair.start()

    def step_across():
        with_pair.wait_recv()
        kind = code[mine]
        from_pair = (kind > 0.5) & (kind < jnp.where(core == 1, 9.0, 1.5))
        comb[...] = jnp.where(from_pair, w_pair[mine], w_me[mine])
        across.start()

    def step_pass():
        across.wait_recv()
        pass_on.start()

    def step_u():
        load_l.wait()
        pass_other = swap(2, m_far.at[mine], m_far.at[mine], pair)
        pass_other.wait_recv()
        kind = code[...]
        picked = jnp.where(kind < 0.5, w_me[...], jnp.where(kind < 1.5, w_pair[...], m_far[...]))
        u_ref[...] = jnp.dot(
            l_inverse[...], picked, precision=lax.Precision.HIGHEST, preferred_element_type=jnp.float32
        )

        @pl.when(r == 0)
        def _():
            top[...] = mat[pl.ds(0, nb)]

        @pl.when(r == 1)
        def _():
            top[...] = w_pair[...]

        @pl.when(r >= 2)
        def _():
            top[...] = m_far[...]

        @pl.when(source)
        def _():
            top[:, :width] = w_me[:, :width]

    depth = hops(core, yh, z, x)
    leaf = expect == 2
    scale = CHUNKS // 8
    late = (x == 0) & (z == 0)
    at_across = jnp.where(late, CHUNKS, jnp.where(depth <= 1, scale, 0))
    at_pass = jnp.where(
        late, CHUNKS, jnp.maximum(0, scale * 7 - (scale * 3) // 2 * (depth - 1))
    )
    at_u = jnp.where(leaf & (depth >= 5), CHUNKS // 2, CHUNKS)

    @pl.when(jnp.logical_not(source))
    def _():
        @pl.loop(0, CHUNKS)
        def _(j):
            pl.when(j == at_across)(step_across)
            pl.when(j == at_pass)(step_pass)
            pl.when(j == at_u)(step_u)
            forward(j, 0).wait_recv()
            send(j)

    pl.when(at_across == CHUNKS)(step_across)
    pl.when(at_pass == CHUNKS)(step_pass)
    pl.when(at_u == CHUNKS)(step_u)

    with_pair.wait_send()
    across.wait_send()
    pass_on.wait_send()
    for k in range(SLOTS):
        @pl.when(kids[k][0])
        def _():
            pltpu.make_async_remote_copy(
                src_ref=panel, dst_ref=panel, send_sem=send_sem.at[k], recv_sem=recv_sem.at[0],
                device_id={"row": r, "col": kids[k][1]}, device_id_type=pl.DeviceIdType.MESH,
            ).wait_send()


def finish_kernel(
    pivots, work_in, panel, u_ref, top,
    out_hbm, u_out, moved, mat, u_half, out_sem, u_sem,
):
    del work_in
    rows = out_hbm.shape[0]
    tile = rows // TILES
    nb, cols = u_ref.shape
    width = panel.shape[1]
    row_count = lax.axis_size("row")
    me = lax.axis_index("row")
    owns_panel = lax.axis_index("col") == 0

    def piece(t):
        return pl.ds(pl.multiple_of(t * tile, tile), tile)

    def store(t):
        return pltpu.make_async_copy(mat.at[piece(t)], out_hbm.at[piece(t)], out_sem.at[t])

    def target(i, other):
        p = pivots[i]
        own, local = local_row(p, nb, row_count)
        return jnp.where((own == me) & (p >= nb), local, other)

    give_u = pltpu.make_async_copy(u_ref, u_out, u_sem.at[0])
    give_u.start()
    u_half[...] = u_ref[...].astype(u_half.dtype)
    mat[pl.ds(rows + 8, 8)] = jnp.zeros((8, cols), mat.dtype)

    @pl.loop(0, nb // 8)
    def _(g):
        for s in range(8):
            i = g * 8 + s
            mat[pl.ds(target(i, rows), 1)] = top[pl.ds(i, 1)]

    @pl.loop(0, TILES)
    def _(t):
        at = piece(t)
        old = mat[at]
        new = old - jnp.dot(panel[at], u_half[...], preferred_element_type=jnp.float32)
        new = jnp.where((t == 0) & (me == 0), u_ref[...], new)
        mat[at, :width] = jnp.where(owns_panel, old[:, :width], new[:, :width])
        mat[at, width:] = new[:, width:]
        store(t).start()

    @pl.loop(0, nb // 8)
    def _(g):
        for s in range(8):
            i = g * 8 + s
            moved[pl.ds(i, 1)] = mat[pl.ds(target(i, rows + 8), 1)]

    for t in range(TILES):
        store(t).wait()
    give_u.wait()


def body(matrix, pivots, l_inverse):
    rows, cols = matrix.shape
    nb = l_inverse.shape[0]
    f32, bf16 = jnp.float32, jnp.bfloat16
    vmem = pl.BlockSpec(memory_space=pltpu.VMEM)
    smem = pl.BlockSpec(memory_space=pltpu.SMEM)
    hbm = pl.BlockSpec(memory_space=pltpu.HBM)
    shape = jax.ShapeDtypeStruct
    panel, work, u_rows, top = pl.pallas_call(
        move_kernel,
        out_shape=(
            shape((rows, nb), bf16), shape((rows + 16, cols), f32),
            shape((nb, cols), f32), shape((nb, cols), f32),
        ),
        in_specs=[smem, vmem, hbm, hbm],
        out_specs=[vmem] * 4,
        scratch_shapes=[
            pltpu.VMEM((nb, cols), f32),
            pltpu.VMEM((nb, cols), f32),
            pltpu.VMEM((nb, cols), f32),
            pltpu.VMEM((nb // 2, cols), f32),
            pltpu.VMEM((nb, 1), f32),
            pltpu.VMEM((nb, nb), f32),
            pltpu.SemaphoreType.DMA((TILES + 1,)),
            pltpu.SemaphoreType.DMA((CHUNKS,)),
            pltpu.SemaphoreType.DMA((SLOTS,)),
            pltpu.SemaphoreType.DMA((3,)),
            pltpu.SemaphoreType.DMA((3,)),
        ],
        compiler_params=pltpu.CompilerParams(
            collective_id=0, has_side_effects=True, vmem_limit_bytes=MOVE_VMEM
        ),
        name="move",
    )(pivots, pivots.reshape(1, nb), matrix, l_inverse)
    out, u_block, moved, _ = pl.pallas_call(
        finish_kernel,
        out_shape=(
            shape((rows, cols), f32), shape((nb, cols), f32), shape((nb, cols), f32),
            shape((rows + 16, cols), f32),
        ),
        in_specs=[smem] + [vmem] * 4,
        out_specs=[hbm, hbm, vmem, vmem],
        scratch_shapes=[
            pltpu.VMEM((nb, cols), bf16),
            pltpu.SemaphoreType.DMA((TILES,)),
            pltpu.SemaphoreType.DMA((1,)),
        ],
        input_output_aliases={1: 3},
        compiler_params=pltpu.CompilerParams(vmem_limit_bytes=FINISH_VMEM),
        name="finish",
    )(pivots, work, panel, u_rows, top)
    return out, u_block, moved


def solution(mesh):
    return jax.shard_map(
        body,
        mesh=mesh,
        in_specs=(P("row", "col"), P(), P()),
        out_specs=(P("row", "col"), P(None, "col"), P("row", "col")),
        check_vma=False,
    )
```

time: 55.6 us -> 47.4 us (0.85)
  the two profiles are of different devices: /device:TPU:156 before, /device:TPU:16 now
where the time goes in v2:
time: 47.4 us; the launch traced here: 47.2 us
  Pallas kernels  42.8 us (90%)
  local copies, waits for them, and re-layouts  3.81 us (8%)
  between operations  0.65 us (1%)
    pallas_call x1, Pallas kernels, body(): pl.pallas_call(move_kernel, out_shape=(shape((rows, nb), bf16), shape((ro...  36.3 us
    pallas_call x1, Pallas kernels, body(): pl.pallas_call(finish_kernel, out_shape=(shape((rows, cols), f32), shape(...  6.49 us
    unnamed x6, local copies, waits for them, and re-layouts  3.81 us

profile of v2, /device:TPU:16, one launch (start us, length us, event | category | flops | bytes accessed | tf_op | source)
XLA Modules:
  0.0 47.2 jit_solution(17424383023157943441)
XLA Ops:
  0.6 0.0 copy-start
  0.6 2.2 %copy-done = f32[2048,512]{1,0:T(8,128)S(1)} copy-done((f32[2048,512]{1,0:T(8,128)S(1)}, f32[2048,512]{1,0:T(8,128)}, u32[]{:S(2)}) %copy-start) | copy-done | bytes 4194328
  2.8 0.0 copy-start.1
  2.8 0.9 %copy-done.1 = f32[256,256]{1,0:T(8,128)S(1)} copy-done((f32[256,256]{1,0:T(8,128)S(1)}, f32[256,256]{1,0:T(8,128)}, u32[]{:S(2)}) %copy-start.1) | copy-done | bytes 262168
  3.8 0.0 copy-start.2
  3.8 0.7 %copy-done.2 = s32[256]{0:T(256)S(1)} copy-done((s32[256]{0:T(256)S(1)}, s32[256]{0:T(256)}, u32[]{:S(2)}) %copy-start.2) | copy-done | bytes 1048
  4.4 36.3 %move.1 = (bf16[2048,256]{1,0:T(8,128)(2,1)S(1)}, f32[2064,512]{1,0:T(8,128)S(1)}, f32[256,512]{1,0:T(8,128)S(1)}, f32[256,512]{1,0:T(8,128)S(1)}) custom-call(s32[256]{0:T(256)S(1)} %copy-done.2, s32[1,256]{1,0:T(1,128)S(1)} %bitcast.1, f32[2048,512]{1,0:T(8,128)S(1)} %copy-done, f32[256,256]{1,0:T(8,128)S(1)} %copy-done.1), custom_call_target="tpu_custom_call" | custom-call | tf_op jit(solution)/shard_map/move/pallas_call | solution.py:325
  40.7 6.5 %finish.1 = (f32[2048,512]{1,0:T(8,128)}, f32[256,512]{1,0:T(8,128)}, f32[256,512]{1,0:T(8,128)}, f32[2064,512]{1,0:T(8,128)S(1)}) custom-call(s32[256]{0:T(256)S(1)} %copy-done.2, f32[2064,512]{1,0:T(8,128)S(1)} %get-tuple-element.10.work_in, bf16[2048,256]{1,0:T(8,128)(2,1)S(1)} %get-tuple-element.11.panel, ...), custom_call_target="tpu_custom_call", output_to_operand_aliasing={{3}: (1, {})} | custom-call | tf_op jit(solution)/shard_map/finish/pallas_call | solution.py:351
Async XLA Ops:
  0.6 2.2 %copy-start = (f32[2048,512]{1,0:T(8,128)S(1)}, f32[2048,512]{1,0:T(8,128)}, u32[]{:S(2)}) copy-start(f32[2048,512]{1,0:T(8,128)} %mat_hbm.1) | copy-start | bytes 12582916
  2.8 0.9 %copy-start.1 = (f32[256,256]{1,0:T(8,128)S(1)}, f32[256,256]{1,0:T(8,128)}, u32[]{:S(2)}) copy-start(f32[256,256]{1,0:T(8,128)} %l_hbm.1) | copy-start | bytes 786436
  3.8 0.7 %copy-start.2 = (s32[256]{0:T(256)S(1)}, s32[256]{0:T(256)}, u32[]{:S(2)}) copy-start(s32[256]{0:T(256)} %pivots.3) | copy-start | bytes 3076

commit v3 on v2

v3 whole, which is shorter than its diff:
```python
import jax
import jax.numpy as jnp
from jax import lax
from jax.experimental import pallas as pl
from jax.experimental.pallas import tpu as pltpu
from jax.sharding import PartitionSpec as P

CHUNKS = 32
TILES = 8
SLOTS = 4
MOVE_VMEM = 24 * 2**20
FINISH_VMEM = 8 * 2**20
NZ = 8
NX = 4


def pick(cond, a, b):
    return jnp.where(cond, a, b)


def column(yh, z, x):
    return (yh * NZ + z) * NX + x


def tree(core, yh, z, x):
    first = core == 0
    root = (yh == 0) & (x == 0)
    flat = z == 0
    up = (z >= 1) & (z <= 3)
    down = (z == 6) | (z == 7)
    step = pick(up, z + 1, z - 1)
    a0 = pick(first, jnp.logical_not(root), root)
    v0 = (flat | up | down) & a0
    k0 = column(yh, pick(flat, 1, step), x)
    inplane = pick(first, flat, jnp.logical_not(flat))
    zlow = flat & a0
    s1x = inplane & (x <= 1)
    v1 = s1x
    k1 = column(yh, z, x + 1)
    wrap = inplane & (x == 0)
    back = first & (yh == 0) & (x == 1) & jnp.logical_not(flat)
    drop = jnp.logical_not(first) & (z == 1) & jnp.logical_not(root)
    v2 = wrap | back
    k2 = column(yh, z, pick(wrap, 3, 0))
    cross = inplane & root
    v3 = cross | zlow | drop
    k3 = pick(cross, column(1, z, x), column(yh, pick(drop, 0, 7), x))
    kids = ((v0, k0), (v1, k1), (v2, k2), (v3, k3))
    zback = pick(z <= 4, z - 1, (z + 1) % NZ)
    px = pick(x == 2, 1, 0)
    inparent = pick(x == 0, column(0, z, 0), column(yh, z, px))
    p_first = pick(
        flat, inparent, pick(root, column(0, z, 1), column(yh, zback, x))
    )
    p_second = pick(
        root, column(0, zback, 0), pick(flat, column(yh, 1, x), inparent)
    )
    return kids, pick(first, p_first, p_second)


def place():
    r = lax.axis_index("row")
    c = lax.axis_index("col")
    return r, c, r % 2, r // 2, c // (NX * NZ), (c // NX) % NZ, c % NX


def hops(core, yh, z, x):
    dz = jnp.minimum(z, NZ - z)
    dx = jnp.minimum(x, NX - x)
    root = (yh == 0) & (x == 0)
    flat = z == 0
    around = pick(core == 0, root & jnp.logical_not(flat), flat & jnp.logical_not(root))
    return dz + dx + yh + pick(around, 2, 0)


def local_row(p, nb, row_count):
    shift = nb.bit_length() - 1
    deal = row_count.bit_length() - 1
    block = jnp.right_shift(p, shift)
    owner = block & (row_count - 1)
    local = jnp.left_shift(jnp.right_shift(block, deal), shift) + (p & (nb - 1))
    return owner, local


def move_kernel(
    pivots_hbm, row_hbm, mat_hbm, l_hbm, mat, u_ref,
    panel, w_me, w_pair, m_far, comb, code, l_inverse, pivot_row, u_half, top, parts, pivots,
    in_sem, recv_sem, send_sem, x_send, x_recv,
):
    r, c, core, yl, yh, z, x = place()
    pair = yl * 2 + 1 - core
    far = (1 - yl) * 2 + core
    source = c == 0
    other = jnp.logical_not(source)
    kids, parent = tree(core, yh, z, x)
    rows, cols = mat_hbm.shape
    tile = rows // TILES
    chunk = rows // CHUNKS
    per = CHUNKS // TILES
    nb, width = l_hbm.shape
    half = nb // 2
    row_count = lax.axis_size("row")

    def load(t):
        at = pl.ds(pl.multiple_of(t * tile, tile), tile)
        return pltpu.make_async_copy(mat_hbm.at[at], mat.at[at], in_sem.at[t])

    def forward(j, k):
        at = pl.ds(pl.multiple_of(j * chunk, chunk), chunk)
        return pltpu.make_async_remote_copy(
            src_ref=panel.at[at],
            dst_ref=panel.at[at],
            send_sem=send_sem.at[k],
            recv_sem=recv_sem.at[j],
            device_id={"row": r, "col": kids[k][1]},
            device_id_type=pl.DeviceIdType.MESH,
        )

    def send(j):
        for k in range(SLOTS):
            @pl.when(kids[k][0])
            def _():
                forward(j, k).start()

    def swap(step, src, dst, to):
        return pltpu.make_async_remote_copy(
            src_ref=src, dst_ref=dst, send_sem=x_send.at[step], recv_sem=x_recv.at[step],
            device_id={"row": to, "col": c}, device_id_type=pl.DeviceIdType.MESH,
        )

    def signal(row, col):
        pl.semaphore_signal(
            barrier, inc=1, device_id={"row": row, "col": col}, device_id_type=pl.DeviceIdType.MESH
        )

    mine = pl.ds(pl.multiple_of(core * half, half), half)
    with_pair = swap(0, w_me, w_pair, pair)
    across = swap(1, comb, m_far.at[mine], far)
    pass_on = swap(2, m_far.at[mine], m_far.at[mine], pair)

    barrier = pltpu.get_barrier_semaphore()

    @pl.when(other)
    def _():
        signal(r, parent)

    signal(pair, c)
    signal(far, c)
    load_p = pltpu.make_async_copy(pivots_hbm, pivots, in_sem.at[TILES])
    load_q = pltpu.make_async_copy(row_hbm, pivot_row, in_sem.at[TILES + 1])
    load_l = pltpu.make_async_copy(l_hbm, l_inverse, in_sem.at[TILES + 2])
    load(0).start()
    load_p.start()
    load_q.start()
    for t in range(1, TILES):
        load(t).start()
    load_l.start()

    expect = 2
    for k in range(SLOTS):
        expect = expect + kids[k][0].astype(jnp.int32)
    pl.semaphore_wait(barrier, expect)

    @pl.when(source)
    def _():
        @pl.loop(0, TILES)
        def _(t):
            load(t).wait()
            at = pl.ds(pl.multiple_of(t * tile, tile), tile)
            panel[at] = mat[at, :width].astype(panel.dtype)
            for s in range(per):
                send(t * per + s)

    @pl.when(other)
    def _():
        @pl.loop(0, TILES)
        def _(t):
            load(t).wait()

    load_p.wait()

    @pl.loop(0, nb // 8)
    def _(g):
        for s in range(8):
            i = g * 8 + s
            own, local = local_row(pivots[i], nb, row_count)
            w_me[pl.ds(i, 1)] = mat[pl.ds(jnp.where(own == r, local, i), 1)]

    with_pair.start()

    load_q.wait()
    owner, local = local_row(pivot_row[...], nb, row_count)
    kind = jnp.where(owner == r, 0.0, jnp.where(owner == pair, 1.0, 2.0))
    down = lax.broadcasted_iota(jnp.int32, (nb, nb), 0)
    along = lax.broadcasted_iota(jnp.int32, (nb, nb), 1)
    spread = jnp.where(down == along, jnp.broadcast_to(kind, (nb, nb)), 0.0)
    code[...] = jnp.sum(spread, axis=1, keepdims=True)
    pivot_row[...] = jnp.where((owner == r) & (pivot_row[...] >= nb), local, rows)

    def step_across():
        with_pair.wait_recv()
        kind = code[mine]
        from_pair = (kind > 0.5) & (kind < jnp.where(core == 1, 9.0, 1.5))
        comb[...] = jnp.where(from_pair, w_pair[mine], w_me[mine])
        across.start()

    def step_pass():
        across.wait_recv()
        pass_on.start()

    def step_u():
        load_l.wait()
        pass_on.wait_recv()
        kind = code[...]
        picked = jnp.where(kind < 0.5, w_me[...], jnp.where(kind < 1.5, w_pair[...], m_far[...]))
        u = jnp.dot(
            l_inverse[...], picked, precision=lax.Precision.HIGHEST, preferred_element_type=jnp.float32
        )
        u_ref[...] = u
        u_half[...] = u.astype(u_half.dtype)

        @pl.when(r == 0)
        def _():
            top[...] = mat[pl.ds(0, nb)]

        @pl.when(r == 1)
        def _():
            top[...] = w_pair[...]

        @pl.when(r >= 2)
        def _():
            top[...] = m_far[...]

        @pl.when(source)
        def _():
            top[:, :width] = w_me[:, :width]

        whole = top[...]
        edge = float(jnp.finfo(jnp.bfloat16).max)
        for p in range(3):
            part = jnp.clip(whole, -edge, edge).astype(jnp.bfloat16)
            parts[p] = part
            whole = whole - part.astype(jnp.float32)

        @pl.loop(0, TILES)
        def _(t):
            at = pl.ds(pl.multiple_of(t * tile, tile), tile)
            place = lax.broadcasted_iota(jnp.int32, (tile, nb), 0) + t * tile
            onehot = jnp.where(place == pivot_row[...], 1.0, 0.0)
            hit = jnp.max(onehot, axis=1, keepdims=True) > 0.5
            onehot = onehot.astype(jnp.bfloat16)
            rows_in = jnp.zeros((tile, cols), jnp.float32)
            for p in (2, 1, 0):
                rows_in += jnp.dot(onehot, parts[p], preferred_element_type=jnp.float32)
            mat[at] = jnp.where(hit, rows_in, mat[at])

    def update(j, size):
        at = pl.ds(pl.multiple_of(j * size, size), size)
        is_top = (r == 0) & (j < nb // size)

        @pl.when(is_top & other)
        def _():
            mat[at] = u_ref[pl.ds(pl.multiple_of((j % (nb // size)) * size, size), size)]

        @pl.when(is_top & source)
        def _():
            mat[at, width:] = u_ref[pl.ds(pl.multiple_of((j % (nb // size)) * size, size), size), width:]

        @pl.when(jnp.logical_not(is_top) & other)
        def _():
            mat[at] = mat[at] - jnp.dot(panel[at], u_half[...], preferred_element_type=jnp.float32)

        @pl.when(jnp.logical_not(is_top) & source)
        def _():
            mat[at, width:] = mat[at, width:] - jnp.dot(
                panel[at], u_half[:, width:], preferred_element_type=jnp.float32
            )

    depth = hops(core, yh, z, x)
    leaf = expect == 2
    early = leaf & (depth >= 5)
    scale = CHUNKS // 8
    late = (yh == 1) & (x == 0) & (z == 0)
    first_go = pick(late, pick(core == 0, CHUNKS, scale * 5), pick(depth <= 1, scale, 0))
    pass_go = jnp.maximum(0, scale * 7 - (scale * 3) // 2 * (depth - 1))
    at_across = pick(source, CHUNKS, first_go)
    at_pass = pick(source | late, CHUNKS, pick(early, 0, pass_go))
    at_u = pick(early, 0, CHUNKS)

    @pl.loop(pick(source, CHUNKS, 0), CHUNKS + 1)
    def _(j):
        pl.when(j == at_across)(step_across)
        pl.when(j == at_pass)(step_pass)
        pl.when(j == at_u)(step_u)

        @pl.when(j < CHUNKS)
        def _():
            forward(j, 0).wait_recv()
            send(j)

            @pl.when(early)
            def _():
                update(j, chunk)

    @pl.when(jnp.logical_not(early))
    def _():
        @pl.loop(0, TILES)
        def _(t):
            update(t, tile)

    with_pair.wait_send()
    across.wait_send()
    pass_on.wait_send()
    for k in range(SLOTS):
        @pl.when(kids[k][0])
        def _():
            pltpu.make_async_remote_copy(
                src_ref=panel, dst_ref=panel, send_sem=send_sem.at[k], recv_sem=recv_sem.at[0],
                device_id={"row": r, "col": kids[k][1]}, device_id_type=pl.DeviceIdType.MESH,
            ).wait_send()


def finish_kernel(pivots_hbm, mat, u_ref, out, u_out, moved_out, moved, pivots, sem):
    rows = out.shape[0]
    tile = rows // TILES
    nb = u_ref.shape[0]
    row_count = lax.axis_size("row")
    me = lax.axis_index("row")
    load_p = pltpu.make_async_copy(pivots_hbm, pivots, sem.at[TILES])
    load_p.start()
    copies = [
        pltpu.make_async_copy(mat.at[pl.ds(t * tile, tile)], out.at[pl.ds(t * tile, tile)], sem.at[t])
        for t in range(TILES)
    ]
    copies.append(pltpu.make_async_copy(u_ref, u_out, sem.at[TILES + 1]))
    for copy in copies:
        copy.start()
    load_p.wait()

    @pl.loop(0, nb // 8)
    def _(g):
        for s in range(8):
            i = g * 8 + s
            p = pivots[i]
            own, local = local_row(p, nb, row_count)
            land = (own == me) & (p >= nb)
            row = mat[pl.ds(jnp.where(land, local, 0), 1)]
            moved[pl.ds(i, 1)] = jnp.where(land, row, jnp.zeros_like(row))

    last = pltpu.make_async_copy(moved, moved_out, sem.at[TILES + 2])
    last.start()
    copies.append(last)
    for copy in copies:
        copy.wait()


def body(matrix, pivots, l_inverse):
    rows, cols = matrix.shape
    nb = l_inverse.shape[0]
    f32, bf16, i32 = jnp.float32, jnp.bfloat16, jnp.int32
    vmem = pl.BlockSpec(memory_space=pltpu.VMEM)
    hbm = pl.BlockSpec(memory_space=pltpu.HBM)
    shape = jax.ShapeDtypeStruct
    stay = lambda array: pltpu.with_memory_space_constraint(array, pltpu.HBM)
    work, u_rows = pl.pallas_call(
        move_kernel,
        out_shape=(shape((rows, cols), f32), shape((nb, cols), f32)),
        in_specs=[hbm] * 4,
        out_specs=[vmem] * 2,
        scratch_shapes=[
            pltpu.VMEM((rows, nb), bf16),
            pltpu.VMEM((nb, cols), f32),
            pltpu.VMEM((nb, cols), f32),
            pltpu.VMEM((nb, cols), f32),
            pltpu.VMEM((nb // 2, cols), f32),
            pltpu.VMEM((nb, 1), f32),
            pltpu.VMEM((nb, nb), f32),
            pltpu.VMEM((1, nb), i32),
            pltpu.VMEM((nb, cols), bf16),
            pltpu.VMEM((nb, cols), f32),
            pltpu.VMEM((3, nb, cols), bf16),
            pltpu.SMEM((nb,), i32),
            pltpu.SemaphoreType.DMA((TILES + 3,)),
            pltpu.SemaphoreType.DMA((CHUNKS,)),
            pltpu.SemaphoreType.DMA((SLOTS,)),
            pltpu.SemaphoreType.DMA((3,)),
            pltpu.SemaphoreType.DMA((3,)),
        ],
        compiler_params=pltpu.CompilerParams(
            collective_id=0, has_side_effects=True, vmem_limit_bytes=MOVE_VMEM
        ),
        name="move",
    )(stay(pivots), stay(pivots.reshape(1, nb)), stay(matrix), stay(l_inverse))
    return pl.pallas_call(
        finish_kernel,
        out_shape=(shape((rows, cols), f32), shape((nb, cols), f32), shape((nb, cols), f32)),
        in_specs=[hbm, vmem, vmem],
        out_specs=[hbm] * 3,
        scratch_shapes=[
            pltpu.VMEM((nb, cols), f32),
            pltpu.SMEM((nb,), i32),
            pltpu.SemaphoreType.DMA((TILES + 3,)),
        ],
        compiler_params=pltpu.CompilerParams(vmem_limit_bytes=FINISH_VMEM),
        name="finish",
    )(stay(pivots), work, u_rows)


def solution(mesh):
    return jax.shard_map(
        body,
        mesh=mesh,
        in_specs=(P("row", "col"), P(), P()),
        out_specs=(P("row", "col"), P(None, "col"), P("row", "col")),
        check_vma=False,
    )
```

time: 47.4 us -> 41.2 us (0.87)
  the two profiles are of different devices: /device:TPU:16 before, /device:TPU:124 now
where the time goes in v3:
time: 41.2 us; the launch traced here: 41.1 us
  Pallas kernels  40.5 us (98%)
  between operations  0.64 us (2%)
    pallas_call x1, Pallas kernels, body(): pl.pallas_call(move_kernel, out_shape=(shape((rows, cols), f32), shape((n...  37.1 us
    pallas_call x1, Pallas kernels, body(): pl.pallas_call(finish_kernel, out_shape=(shape((rows, cols), f32), shape(...  3.36 us

profile of v3, /device:TPU:124, one launch (start us, length us, event | category | flops | bytes accessed | tf_op | source)
XLA Modules:
  0.0 41.1 jit_solution(15819891504578017010)
XLA Ops:
  0.6 37.1 %move.1 = (f32[2048,512]{1,0:T(8,128)S(1)}, f32[256,512]{1,0:T(8,128)S(1)}) custom-call(s32[256]{0:T(256)} %pivots_hbm.3, s32[1,256]{1,0:T(1,128)} %bitcast.1, f32[2048,512]{1,0:T(8,128)} %mat_hbm.1, f32[256,256]{1,0:T(8,128)} %l_hbm.1), custom_call_target="tpu_custom_call" | custom-call | tf_op jit(solution)/shard_map/move/pallas_call | solution.py:365
  37.8 3.4 %finish.1 = (f32[2048,512]{1,0:T(8,128)}, f32[256,512]{1,0:T(8,128)}, f32[256,512]{1,0:T(8,128)}) custom-call(s32[256]{0:T(256)} %pivots_hbm.3, f32[2048,512]{1,0:T(8,128)S(1)} %get-tuple-element.5.mat, f32[256,512]{1,0:T(8,128)S(1)} %get-tuple-element.6.u_ref), custom_call_target="tpu_custom_call" | custom-call | tf_op jit(solution)/shard_map/finish/pallas_call | solution.py:394

commit v4 on v3

--- a/solution.py
+++ b/solution.py
@@ -8,6 +8,7 @@
 CHUNKS = 32
 TILES = 8
 SLOTS = 4
+PARTS = 3
 MOVE_VMEM = 24 * 2**20
 FINISH_VMEM = 8 * 2**20
 NZ = 8
@@ -83,8 +84,8 @@
 
 
 def move_kernel(
-    pivots_hbm, row_hbm, mat_hbm, l_hbm, mat, u_ref,
-    panel, w_me, w_pair, m_far, comb, code, l_inverse, pivot_row, u_half, top, parts, pivots,
+    row_hbm, mat_hbm, l_hbm, mat, u_ref, takes,
+    panel, w_me, w_pair, m_far, comb, code, l_inverse, pivot_row, u_half, parts, from_row, from_at,
     in_sem, recv_sem, send_sem, x_send, x_recv,
 ):
     r, c, core, yl, yh, z, x = place()
@@ -146,15 +147,26 @@
 
     signal(pair, c)
     signal(far, c)
-    load_p = pltpu.make_async_copy(pivots_hbm, pivots, in_sem.at[TILES])
-    load_q = pltpu.make_async_copy(row_hbm, pivot_row, in_sem.at[TILES + 1])
+    load_p = pltpu.make_async_copy(row_hbm, pivot_row, in_sem.at[TILES])
+    give_p = pltpu.make_async_copy(from_row, from_at, in_sem.at[TILES + 1])
     load_l = pltpu.make_async_copy(l_hbm, l_inverse, in_sem.at[TILES + 2])
+    load_p.start()
     load(0).start()
-    load_p.start()
-    load_q.start()
     for t in range(1, TILES):
         load(t).start()
     load_l.start()
+
+    load_p.wait()
+    owner, local = local_row(pivot_row[...], nb, row_count)
+    from_row[...] = jnp.where(owner == r, local, lax.broadcasted_iota(jnp.int32, (1, nb), 1))
+    takes[...] = jnp.where((owner == r) & (pivot_row[...] >= nb), local, rows)
+    mat[pl.ds(rows, 8)] = jnp.zeros((8, cols), mat.dtype)
+    kind = jnp.where(owner == r, 0.0, jnp.where(owner == pair, 1.0, 2.0))
+    down = lax.broadcasted_iota(jnp.int32, (nb, nb), 0)
+    along = lax.broadcasted_iota(jnp.int32, (nb, nb), 1)
+    spread = jnp.where(down == along, jnp.broadcast_to(kind, (nb, nb)), 0.0)
+    code[...] = jnp.sum(spread, axis=1, keepdims=True)
+    give_p.start()
 
     expect = 2
     for k in range(SLOTS):
@@ -177,25 +189,16 @@
         def _(t):
             load(t).wait()
 
-    load_p.wait()
+    give_p.wait()
 
     @pl.loop(0, nb // 8)
     def _(g):
+        out = w_me.at[pl.ds(pl.multiple_of(g * 8, 8), 8)]
+        got = [mat[pl.ds(from_at[0, g * 8 + s], 1)] for s in range(8)]
         for s in range(8):
-            i = g * 8 + s
-            own, local = local_row(pivots[i], nb, row_count)
-            w_me[pl.ds(i, 1)] = mat[pl.ds(jnp.where(own == r, local, i), 1)]
+            out[pl.ds(s, 1)] = got[s]
 
     with_pair.start()
-
-    load_q.wait()
-    owner, local = local_row(pivot_row[...], nb, row_count)
-    kind = jnp.where(owner == r, 0.0, jnp.where(owner == pair, 1.0, 2.0))
-    down = lax.broadcasted_iota(jnp.int32, (nb, nb), 0)
-    along = lax.broadcasted_iota(jnp.int32, (nb, nb), 1)
-    spread = jnp.where(down == along, jnp.broadcast_to(kind, (nb, nb)), 0.0)
-    code[...] = jnp.sum(spread, axis=1, keepdims=True)
-    pivot_row[...] = jnp.where((owner == r) & (pivot_row[...] >= nb), local, rows)
 
     def step_across():
         with_pair.wait_recv()
@@ -219,40 +222,30 @@
         u_ref[...] = u
         u_half[...] = u.astype(u_half.dtype)
 
-        @pl.when(r == 0)
-        def _():
-            top[...] = mat[pl.ds(0, nb)]
-
-        @pl.when(r == 1)
-        def _():
-            top[...] = w_pair[...]
-
-        @pl.when(r >= 2)
-        def _():
-            top[...] = m_far[...]
+        def split(at, whole):
+            edge = float(jnp.finfo(jnp.bfloat16).max)
+            for p in range(PARTS):
+                part = jnp.clip(whole, -edge, edge).astype(jnp.bfloat16)
+                parts[pl.ds(p * nb, nb), at] = part
+                whole = whole - part.astype(jnp.float32)
+
+        whole = jnp.where(r == 0, mat[pl.ds(0, nb)], jnp.where(r == 1, w_pair[...], m_far[...]))
+        split(pl.ds(0, cols), whole)
 
         @pl.when(source)
         def _():
-            top[:, :width] = w_me[:, :width]
-
-        whole = top[...]
-        edge = float(jnp.finfo(jnp.bfloat16).max)
-        for p in range(3):
-            part = jnp.clip(whole, -edge, edge).astype(jnp.bfloat16)
-            parts[p] = part
-            whole = whole - part.astype(jnp.float32)
-
-        @pl.loop(0, TILES)
-        def _(t):
-            at = pl.ds(pl.multiple_of(t * tile, tile), tile)
-            place = lax.broadcasted_iota(jnp.int32, (tile, nb), 0) + t * tile
-            onehot = jnp.where(place == pivot_row[...], 1.0, 0.0)
-            hit = jnp.max(onehot, axis=1, keepdims=True) > 0.5
-            onehot = onehot.astype(jnp.bfloat16)
-            rows_in = jnp.zeros((tile, cols), jnp.float32)
-            for p in (2, 1, 0):
-                rows_in += jnp.dot(onehot, parts[p], preferred_element_type=jnp.float32)
-            mat[at] = jnp.where(hit, rows_in, mat[at])
+            split(pl.ds(0, width), w_me[:, :width])
+
+    def step_swap(t):
+        at = pl.ds(pl.multiple_of(t * tile, tile), tile)
+        index = lax.broadcasted_iota(jnp.int32, (tile, nb), 0) + t * tile
+        onehot = jnp.where(index == takes[...], 1.0, 0.0)
+        hit = jnp.max(onehot, axis=1, keepdims=True) > 0.5
+        onehot = onehot.astype(jnp.bfloat16)
+        rows_in = jnp.dot(
+            jnp.concatenate([onehot] * PARTS, axis=1), parts[...], preferred_element_type=jnp.float32
+        )
+        mat[at] = jnp.where(hit, rows_in, mat[at])
 
     def update(j, size):
         at = pl.ds(pl.multiple_of(j * size, size), size)
@@ -278,35 +271,40 @@
 
     depth = hops(core, yh, z, x)
     leaf = expect == 2
-    early = leaf & (depth >= 5)
+    free = leaf | source | (depth >= 6)
     scale = CHUNKS // 8
+    swapped = 1 + 2 * TILES
     late = (yh == 1) & (x == 0) & (z == 0)
-    first_go = pick(late, pick(core == 0, CHUNKS, scale * 5), pick(depth <= 1, scale, 0))
+    late_go = pick(core == 0, CHUNKS - scale // 2, scale * 5)
+    at_across = pick(late, late_go, pick((depth <= 1) & other, scale, 0))
     pass_go = jnp.maximum(0, scale * 7 - (scale * 3) // 2 * (depth - 1))
-    at_across = pick(source, CHUNKS, first_go)
-    at_pass = pick(source | late, CHUNKS, pick(early, 0, pass_go))
-    at_u = pick(early, 0, CHUNKS)
-
-    @pl.loop(pick(source, CHUNKS, 0), CHUNKS + 1)
+    at_pass = pick(late, pick(core == 0, CHUNKS, scale * 5 + 1), pick(free, 0, pass_go))
+    at_u = pick(late, at_pass + 1, pick(free, 0, CHUNKS))
+
+    @pl.loop(0, jnp.maximum(CHUNKS, at_u + swapped + CHUNKS // 2))
     def _(j):
         pl.when(j == at_across)(step_across)
         pl.when(j == at_pass)(step_pass)
-        pl.when(j == at_u)(step_u)
-
-        @pl.when(j < CHUNKS)
+
+        q = j - at_u
+        pl.when(q == 0)(step_u)
+
+        @pl.when((j < CHUNKS) & other)
         def _():
             forward(j, 0).wait_recv()
             send(j)
 
-            @pl.when(early)
-            def _():
-                update(j, chunk)
-
-    @pl.when(jnp.logical_not(early))
-    def _():
-        @pl.loop(0, TILES)
-        def _(t):
-            update(t, tile)
+        @pl.when((q > 0) & (q < swapped) & (q % 2 == 0))
+        def _():
+            step_swap(q // 2 - 1)
+
+        @pl.when(q >= swapped)
+        def _():
+            k = (q - swapped) * 2
+
+            @pl.loop(jnp.minimum(k, j), jnp.minimum(jnp.minimum(k + 2, j + 1), CHUNKS))
+            def _(i):
+                update(i, chunk)
 
     with_pair.wait_send()
     across.wait_send()
@@ -320,14 +318,12 @@
             ).wait_send()
 
 
-def finish_kernel(pivots_hbm, mat, u_ref, out, u_out, moved_out, moved, pivots, sem):
+def finish_kernel(mat, u_ref, takes, out, u_out, moved_out, moved, takes_at, sem):
     rows = out.shape[0]
     tile = rows // TILES
     nb = u_ref.shape[0]
-    row_count = lax.axis_size("row")
-    me = lax.axis_index("row")
-    load_p = pltpu.make_async_copy(pivots_hbm, pivots, sem.at[TILES])
-    load_p.start()
+    give_t = pltpu.make_async_copy(takes, takes_at, sem.at[TILES])
+    give_t.start()
     copies = [
         pltpu.make_async_copy(mat.at[pl.ds(t * tile, tile)], out.at[pl.ds(t * tile, tile)], sem.at[t])
         for t in range(TILES)
@@ -335,17 +331,14 @@
     copies.append(pltpu.make_async_copy(u_ref, u_out, sem.at[TILES + 1]))
     for copy in copies:
         copy.start()
-    load_p.wait()
+    give_t.wait()
 
     @pl.loop(0, nb // 8)
     def _(g):
+        eight = moved.at[pl.ds(pl.multiple_of(g * 8, 8), 8)]
+        got = [mat[pl.ds(takes_at[0, g * 8 + s], 1)] for s in range(8)]
         for s in range(8):
-            i = g * 8 + s
-            p = pivots[i]
-            own, local = local_row(p, nb, row_count)
-            land = (own == me) & (p >= nb)
-            row = mat[pl.ds(jnp.where(land, local, 0), 1)]
-            moved[pl.ds(i, 1)] = jnp.where(land, row, jnp.zeros_like(row))
+            eight[pl.ds(s, 1)] = got[s]
 
     last = pltpu.make_async_copy(moved, moved_out, sem.at[TILES + 2])
     last.start()
@@ -362,11 +355,11 @@
     hbm = pl.BlockSpec(memory_space=pltpu.HBM)
     shape = jax.ShapeDtypeStruct
     stay = lambda array: pltpu.with_memory_space_constraint(array, pltpu.HBM)
-    work, u_rows = pl.pallas_call(
+    work, u_rows, takes = pl.pallas_call(
         move_kernel,
-        out_shape=(shape((rows, cols), f32), shape((nb, cols), f32)),
-        in_specs=[hbm] * 4,
-        out_specs=[vmem] * 2,
+        out_shape=(shape((rows + 8, cols), f32), shape((nb, cols), f32), shape((1, nb), i32)),
+        in_specs=[hbm] * 3,
+        out_specs=[vmem] * 3,
         scratch_shapes=[
             pltpu.VMEM((rows, nb), bf16),
             pltpu.VMEM((nb, cols), f32),
@@ -377,9 +370,9 @@
             pltpu.VMEM((nb, nb), f32),
             pltpu.VMEM((1, nb), i32),
             pltpu.VMEM((nb, cols), bf16),
-            pltpu.VMEM((nb, cols), f32),
-            pltpu.VMEM((3, nb, cols), bf16),
-            pltpu.SMEM((nb,), i32),
+            pltpu.VMEM((PARTS * nb, cols), bf16),
+            pltpu.VMEM((1, nb), i32),
+            pltpu.SMEM((1, nb), i32),
             pltpu.SemaphoreType.DMA((TILES + 3,)),
             pltpu.SemaphoreType.DMA((CHUNKS,)),
             pltpu.SemaphoreType.DMA((SLOTS,)),
@@ -390,20 +383,20 @@
             collective_id=0, has_side_effects=True, vmem_limit_bytes=MOVE_VMEM
         ),
         name="move",
-    )(stay(pivots), stay(pivots.reshape(1, nb)), stay(matrix), stay(l_inverse))
+    )(stay(pivots.reshape(1, nb)), stay(matrix), stay(l_inverse))
     return pl.pallas_call(
         finish_kernel,
         out_shape=(shape((rows, cols), f32), shape((nb, cols), f32), shape((nb, cols), f32)),
-        in_specs=[hbm, vmem, vmem],
+        in_specs=[vmem] * 3,
         out_specs=[hbm] * 3,
         scratch_shapes=[
             pltpu.VMEM((nb, cols), f32),
-            pltpu.SMEM((nb,), i32),
+            pltpu.SMEM((1, nb), i32),
             pltpu.SemaphoreType.DMA((TILES + 3,)),
         ],
         compiler_params=pltpu.CompilerParams(vmem_limit_bytes=FINISH_VMEM),
         name="finish",
-    )(stay(pivots), work, u_rows)
+    )(work, u_rows, takes)
 
 
 def solution(mesh):

time: 41.2 us -> 44.8 us (1.087)
  the two profiles are of different devices: /device:TPU:124 before, /device:TPU:92 now
where the time goes in v4:
time: 44.8 us; the launch traced here: 44.7 us
  Pallas kernels  44.1 us (98%)
  between operations  0.64 us (1%)
    pallas_call x1, Pallas kernels, body(): pl.pallas_call(move_kernel, out_shape=(shape((rows + 8, cols), f32), shap...  41.7 us
    pallas_call x1, Pallas kernels, body(): pl.pallas_call(finish_kernel, out_shape=(shape((rows, cols), f32), shape(...  2.43 us

profile of v4, /device:TPU:92, one launch (start us, length us, event | category | flops | bytes accessed | tf_op | source)
XLA Modules:
  0.0 44.7 jit_solution(4186684394257560853)
XLA Ops:
  0.6 41.7 %move.1 = (f32[2056,512]{1,0:T(8,128)S(1)}, f32[256,512]{1,0:T(8,128)S(1)}, s32[1,256]{1,0:T(1,128)S(1)}) custom-call(s32[1,256]{1,0:T(1,128)} %bitcast.1, f32[2048,512]{1,0:T(8,128)} %mat_hbm.1, f32[256,256]{1,0:T(8,128)} %l_hbm.1), custom_call_target="tpu_custom_call" | custom-call | tf_op jit(solution)/shard_map/move/pallas_call | solution.py:358
  42.3 2.4 %finish.1 = (f32[2048,512]{1,0:T(8,128)}, f32[256,512]{1,0:T(8,128)}, f32[256,512]{1,0:T(8,128)}) custom-call(f32[2056,512]{1,0:T(8,128)S(1)} %get-tuple-element.6.mat, f32[256,512]{1,0:T(8,128)S(1)} %get-tuple-element.7.u_ref, s32[1,256]{1,0:T(1,128)S(1)} %get-tuple-element.8.takes), custom_call_target="tpu_custom_call" | custom-call | tf_op jit(solution)/shard_map/finish/pallas_call | solution.py:387

commit v5 on v4

--- a/solution.py
+++ b/solution.py
@@ -9,6 +9,7 @@
 TILES = 8
 SLOTS = 4
 PARTS = 3
+SIDES = 2
 MOVE_VMEM = 24 * 2**20
 FINISH_VMEM = 8 * 2**20
 NZ = 8
@@ -100,6 +101,7 @@
     per = CHUNKS // TILES
     nb, width = l_hbm.shape
     half = nb // 2
+    side = cols // SIDES
     row_count = lax.axis_size("row")
 
     def load(t):
@@ -211,30 +213,31 @@
         across.wait_recv()
         pass_on.start()
 
-    def step_u():
+    def step_wait():
         load_l.wait()
         pass_on.wait_recv()
+
+    def step_u(h):
+        at = pl.ds(pl.multiple_of(h * side, side), side)
         kind = code[...]
-        picked = jnp.where(kind < 0.5, w_me[...], jnp.where(kind < 1.5, w_pair[...], m_far[...]))
+        picked = jnp.where(kind < 0.5, w_me[:, at], jnp.where(kind < 1.5, w_pair[:, at], m_far[:, at]))
         u = jnp.dot(
             l_inverse[...], picked, precision=lax.Precision.HIGHEST, preferred_element_type=jnp.float32
         )
-        u_ref[...] = u
-        u_half[...] = u.astype(u_half.dtype)
-
-        def split(at, whole):
-            edge = float(jnp.finfo(jnp.bfloat16).max)
-            for p in range(PARTS):
-                part = jnp.clip(whole, -edge, edge).astype(jnp.bfloat16)
-                parts[pl.ds(p * nb, nb), at] = part
-                whole = whole - part.astype(jnp.float32)
-
-        whole = jnp.where(r == 0, mat[pl.ds(0, nb)], jnp.where(r == 1, w_pair[...], m_far[...]))
-        split(pl.ds(0, cols), whole)
-
-        @pl.when(source)
-        def _():
-            split(pl.ds(0, width), w_me[:, :width])
+        u_ref[:, at] = u
+        u_half[:, at] = u.astype(u_half.dtype)
+
+    def step_split(h):
+        at = pl.ds(pl.multiple_of(h * side, side), side)
+        whole = jnp.where(
+            r == 0, mat[pl.ds(0, nb), at], jnp.where(r == 1, w_pair[:, at], m_far[:, at])
+        )
+        whole = jnp.where(source & (h * side < width), w_me[:, at], whole)
+        edge = float(jnp.finfo(jnp.bfloat16).max)
+        for p in range(PARTS):
+            part = jnp.clip(whole, -edge, edge).astype(jnp.bfloat16)
+            parts[pl.ds(p * nb, nb), at] = part
+            whole = whole - part.astype(jnp.float32)
 
     def step_swap(t):
         at = pl.ds(pl.multiple_of(t * tile, tile), tile)
@@ -270,41 +273,71 @@
             )
 
     depth = hops(core, yh, z, x)
-    leaf = expect == 2
-    free = leaf | source | (depth >= 6)
     scale = CHUNKS // 8
-    swapped = 1 + 2 * TILES
+    gap = (scale * 3) // 2
     late = (yh == 1) & (x == 0) & (z == 0)
+    compact = (expect == 2) & jnp.logical_not(late)
+    spread_out = jnp.logical_not(compact)
     late_go = pick(core == 0, CHUNKS - scale // 2, scale * 5)
     at_across = pick(late, late_go, pick((depth <= 1) & other, scale, 0))
-    pass_go = jnp.maximum(0, scale * 7 - (scale * 3) // 2 * (depth - 1))
-    at_pass = pick(late, pick(core == 0, CHUNKS, scale * 5 + 1), pick(free, 0, pass_go))
-    at_u = pick(late, at_pass + 1, pick(free, 0, CHUNKS))
-
-    @pl.loop(0, jnp.maximum(CHUNKS, at_u + swapped + CHUNKS // 2))
+    at_pass = pick(late, pick(core == 0, CHUNKS, late_go + 1), jnp.maximum(0, gap * (5 - depth) + 1))
+    at_u = pick(late, at_pass + 1, pick(depth >= 6, 0, gap * (6 - depth) + 1))
+    at_across = pick(source, 0, at_across)
+    at_pass = pick(source, 1, at_pass)
+    at_u = pick(source, 2, at_u)
+    split_at = 4 * SIDES
+    swap_at = split_at + 2 * SIDES
+    steps = swap_at + 2 * TILES
+
+    @pl.when(compact)
+    def _():
+        step_across()
+        step_pass()
+        step_wait()
+
+        @pl.loop(0, SIDES)
+        def _(h):
+            step_u(h)
+            step_split(h)
+
+        @pl.loop(0, TILES)
+        def _(t):
+            step_swap(t)
+
+    @pl.loop(0, pick(compact, CHUNKS, jnp.maximum(CHUNKS, at_u + steps)))
     def _(j):
-        pl.when(j == at_across)(step_across)
-        pl.when(j == at_pass)(step_pass)
-
-        q = j - at_u
-        pl.when(q == 0)(step_u)
+        pl.when(spread_out & (j == at_across))(step_across)
+        pl.when(spread_out & (j == at_pass))(step_pass)
 
         @pl.when((j < CHUNKS) & other)
         def _():
             forward(j, 0).wait_recv()
             send(j)
 
-        @pl.when((q > 0) & (q < swapped) & (q % 2 == 0))
-        def _():
-            step_swap(q // 2 - 1)
-
-        @pl.when(q >= swapped)
-        def _():
-            k = (q - swapped) * 2
-
-            @pl.loop(jnp.minimum(k, j), jnp.minimum(jnp.minimum(k + 2, j + 1), CHUNKS))
-            def _(i):
-                update(i, chunk)
+        @pl.when(compact)
+        def _():
+            update(j, chunk)
+
+        q = j - at_u
+        pl.when(spread_out & (q == 0))(step_wait)
+
+        @pl.when(spread_out & (q >= 0) & (q < split_at) & (q % 4 == 0))
+        def _():
+            step_u(q // 4)
+
+        @pl.when(spread_out & (q >= split_at) & (q < swap_at) & (q % 2 == 0))
+        def _():
+            step_split((q - split_at) // 2)
+
+        @pl.when(spread_out & (q >= swap_at) & (q < steps) & (q % 2 == 0))
+        def _():
+            step_swap((q - swap_at) // 2)
+
+    @pl.when(spread_out)
+    def _():
+        @pl.loop(0, TILES)
+        def _(t):
+            update(t, tile)
 
     with_pair.wait_send()
     across.wait_send()

time: 44.8 us -> 41.2 us (0.920)
  the two profiles are of different devices: /device:TPU:92 before, /device:TPU:16 now
where the time goes in v5:
time: 41.2 us; the launch traced here: 41.1 us
  Pallas kernels  40.5 us (98%)
  between operations  0.64 us (2%)
    pallas_call x1, Pallas kernels, body(): pl.pallas_call(move_kernel, out_shape=(shape((rows + 8, cols), f32), shap...  38.1 us
    pallas_call x1, Pallas kernels, body(): pl.pallas_call(finish_kernel, out_shape=(shape((rows, cols), f32), shape(...  2.43 us

profile of v5, /device:TPU:16, one launch (start us, length us, event | category | flops | bytes accessed | tf_op | source)
XLA Modules:
  0.0 41.1 jit_solution(5239880706799432392)
XLA Ops:
  0.6 38.1 %move.1 = (f32[2056,512]{1,0:T(8,128)S(1)}, f32[256,512]{1,0:T(8,128)S(1)}, s32[1,256]{1,0:T(1,128)S(1)}) custom-call(s32[1,256]{1,0:T(1,128)} %bitcast.1, f32[2048,512]{1,0:T(8,128)} %mat_hbm.1, f32[256,256]{1,0:T(8,128)} %l_hbm.1), custom_call_target="tpu_custom_call" | custom-call | tf_op jit(solution)/shard_map/move/pallas_call | solution.py:391
  38.7 2.4 %finish.1 = (f32[2048,512]{1,0:T(8,128)}, f32[256,512]{1,0:T(8,128)}, f32[256,512]{1,0:T(8,128)}) custom-call(f32[2056,512]{1,0:T(8,128)S(1)} %get-tuple-element.6.mat, f32[256,512]{1,0:T(8,128)S(1)} %get-tuple-element.7.u_ref, s32[1,256]{1,0:T(1,128)S(1)} %get-tuple-element.8.takes), custom_call_target="tpu_custom_call" | custom-call | tf_op jit(solution)/shard_map/finish/pallas_call | solution.py:420

commit v6 on v5

--- a/solution.py
+++ b/solution.py
@@ -202,6 +202,15 @@
 
     with_pair.start()
 
+    def sent():
+        for k in range(SLOTS):
+            @pl.when(kids[k][0])
+            def _():
+                pltpu.make_async_remote_copy(
+                    src_ref=panel, dst_ref=panel, send_sem=send_sem.at[k], recv_sem=recv_sem.at[0],
+                    device_id={"row": r, "col": kids[k][1]}, device_id_type=pl.DeviceIdType.MESH,
+                ).wait_send()
+
     def step_across():
         with_pair.wait_recv()
         kind = code[mine]
@@ -275,13 +284,12 @@
     depth = hops(core, yh, z, x)
     scale = CHUNKS // 8
     gap = (scale * 3) // 2
-    late = (yh == 1) & (x == 0) & (z == 0)
-    compact = (expect == 2) & jnp.logical_not(late)
+    compact = expect == 2
+    arrive = compact & (depth >= 6)
     spread_out = jnp.logical_not(compact)
-    late_go = pick(core == 0, CHUNKS - scale // 2, scale * 5)
-    at_across = pick(late, late_go, pick((depth <= 1) & other, scale, 0))
-    at_pass = pick(late, pick(core == 0, CHUNKS, late_go + 1), jnp.maximum(0, gap * (5 - depth) + 1))
-    at_u = pick(late, at_pass + 1, pick(depth >= 6, 0, gap * (6 - depth) + 1))
+    at_across = pick(depth <= 1, scale, 0)
+    at_pass = jnp.maximum(0, gap * (5 - depth) + 1)
+    at_u = pick(depth >= 6, 0, gap * (6 - depth) + 1)
     at_across = pick(source, 0, at_across)
     at_pass = pick(source, 1, at_pass)
     at_u = pick(source, 2, at_u)
@@ -289,6 +297,8 @@
     swap_at = split_at + 2 * SIDES
     steps = swap_at + 2 * TILES
 
+    pl.when(source)(sent)
+
     @pl.when(compact)
     def _():
         step_across()
@@ -314,7 +324,7 @@
             forward(j, 0).wait_recv()
             send(j)
 
-        @pl.when(compact)
+        @pl.when(arrive)
         def _():
             update(j, chunk)
 
@@ -333,7 +343,7 @@
         def _():
             step_swap((q - swap_at) // 2)
 
-    @pl.when(spread_out)
+    @pl.when(jnp.logical_not(arrive))
     def _():
         @pl.loop(0, TILES)
         def _(t):
@@ -342,13 +352,7 @@
     with_pair.wait_send()
     across.wait_send()
     pass_on.wait_send()
-    for k in range(SLOTS):
-        @pl.when(kids[k][0])
-        def _():
-            pltpu.make_async_remote_copy(
-                src_ref=panel, dst_ref=panel, send_sem=send_sem.at[k], recv_sem=recv_sem.at[0],
-                device_id={"row": r, "col": kids[k][1]}, device_id_type=pl.DeviceIdType.MESH,
-            ).wait_send()
+    pl.when(other)(sent)
 
 
 def finish_kernel(mat, u_ref, takes, out, u_out, moved_out, moved, takes_at, sem):

time: 41.2 us -> 37.7 us (0.915)
  the two profiles are of different devices: /device:TPU:16 before, /device:TPU:1 now
where the time goes in v6:
time: 37.7 us; the launch traced here: 37.6 us
  Pallas kernels  37 us (98%)
  between operations  0.64 us (2%)
    pallas_call x1, Pallas kernels, body(): pl.pallas_call(move_kernel, out_shape=(shape((rows + 8, cols), f32), shap...  34.6 us
    pallas_call x1, Pallas kernels, body(): pl.pallas_call(finish_kernel, out_shape=(shape((rows, cols), f32), shape(...  2.43 us

profile of v6, /device:TPU:1, one launch (start us, length us, event | category | flops | bytes accessed | tf_op | source)
XLA Modules:
  0.0 37.6 jit_solution(610533624627977723)
XLA Ops:
  0.6 34.6 %move.1 = (f32[2056,512]{1,0:T(8,128)S(1)}, f32[256,512]{1,0:T(8,128)S(1)}, s32[1,256]{1,0:T(1,128)S(1)}) custom-call(s32[1,256]{1,0:T(1,128)} %bitcast.1, f32[2048,512]{1,0:T(8,128)} %mat_hbm.1, f32[256,256]{1,0:T(8,128)} %l_hbm.1), custom_call_target="tpu_custom_call" | custom-call | tf_op jit(solution)/shard_map/move/pallas_call | solution.py:395
  35.2 2.4 %finish.1 = (f32[2048,512]{1,0:T(8,128)}, f32[256,512]{1,0:T(8,128)}, f32[256,512]{1,0:T(8,128)}) custom-call(f32[2056,512]{1,0:T(8,128)S(1)} %get-tuple-element.6.mat, f32[256,512]{1,0:T(8,128)S(1)} %get-tuple-element.7.u_ref, s32[1,256]{1,0:T(1,128)S(1)} %get-tuple-element.8.takes), custom_call_target="tpu_custom_call" | custom-call | tf_op jit(solution)/shard_map/finish/pallas_call | solution.py:424

commit v7 on v5

--- a/solution.py
+++ b/solution.py
@@ -8,7 +8,7 @@
 CHUNKS = 32
 TILES = 8
 SLOTS = 4
-PARTS = 3
+PARTS = 2
 SIDES = 2
 MOVE_VMEM = 24 * 2**20
 FINISH_VMEM = 8 * 2**20
@@ -26,53 +26,72 @@
 
 def tree(core, yh, z, x):
     first = core == 0
+    second = jnp.logical_not(first)
     root = (yh == 0) & (x == 0)
+    off = jnp.logical_not(root)
     flat = z == 0
     up = (z >= 1) & (z <= 3)
     down = (z == 6) | (z == 7)
-    step = pick(up, z + 1, z - 1)
-    a0 = pick(first, jnp.logical_not(root), root)
-    v0 = (flat | up | down) & a0
-    k0 = column(yh, pick(flat, 1, step), x)
+    odd = (x % 2) == 1
     inplane = pick(first, flat, jnp.logical_not(flat))
-    zlow = flat & a0
-    s1x = inplane & (x <= 1)
-    v1 = s1x
-    k1 = column(yh, z, x + 1)
-    wrap = inplane & (x == 0)
-    back = first & (yh == 0) & (x == 1) & jnp.logical_not(flat)
-    drop = jnp.logical_not(first) & (z == 1) & jnp.logical_not(root)
-    v2 = wrap | back
-    k2 = column(yh, z, pick(wrap, 3, 0))
-    cross = inplane & root
-    v3 = cross | zlow | drop
-    k3 = pick(cross, column(1, z, x), column(yh, pick(drop, 0, 7), x))
-    kids = ((v0, k0), (v1, k1), (v2, k2), (v3, k3))
-    zback = pick(z <= 4, z - 1, (z + 1) % NZ)
-    px = pick(x == 2, 1, 0)
-    inparent = pick(x == 0, column(0, z, 0), column(yh, z, px))
-    p_first = pick(
-        flat, inparent, pick(root, column(0, z, 1), column(yh, zback, x))
+    twin = first & ((x == 2) | ((yh == 1) & (x == 0)))
+    only = pick(x == 1, 2, 3)
+    along = pick(first, off, root)
+    v0 = along & (flat | up | down | (twin & (z == 5)))
+    k0 = column(yh, pick(flat, 1, pick(up, z + 1, z - 1)), x)
+    c0 = pick(twin & (z == 3), 2, pick(twin & (z == 5), 3, 0))
+    drop = second & (z == 1) & off
+    v2 = (along & flat) | drop
+    k2 = column(yh, pick(drop, 0, 7), x)
+    c2 = pick(twin, 1, 0)
+    back = first & jnp.logical_not(flat) & (yh == 0) & (x == 1)
+    v1 = (inplane & jnp.logical_not((yh == 0) & (x == 2))) | back
+    x1 = pick(odd, 2, pick(x == 2, 1, pick(yh == 0, 1, 3)))
+    k1 = column(yh, z, pick(back, 0, x1))
+    c1 = pick(back | root, 0, pick(odd, only, pick(x == 2, 3, 2)))
+    v3 = inplane & (root | odd)
+    k3 = pick(root, column(0, z, 3), pick(yh == 0, column(1, z, x), column(1, z, 0)))
+    c3 = pick(root, pick(first, 1, 0), only)
+    kids = ((v0, c0, k0), (v1, c1, k1), (v2, c2, k2), (v3, c3, k3))
+    near = pick(z <= 4, z - 1, (z + 1) % NZ)
+    in_a = pick(
+        yh == 0,
+        pick(odd, column(0, z, 0), column(0, z, 1)),
+        pick(x == 1, column(0, z, 1), pick(x == 3, column(1, z, 0), column(1, z, 1))),
     )
-    p_second = pick(
-        root, column(0, zback, 0), pick(flat, column(yh, 1, x), inparent)
+    in_b = pick(
+        yh == 0,
+        pick(odd, column(0, z, 0), column(0, z, 3)),
+        pick(x == 1, column(1, z, 2), pick(x == 3, column(0, z, 3), column(1, z, 3))),
     )
-    return kids, pick(first, p_first, p_second)
+    chain_a = pick(root, column(0, z, 1), column(yh, near, x))
+    chain_b = pick(twin & (z == 4), column(yh, 5, x), chain_a)
+    stem = pick(root, column(0, near, 0), column(yh, 1, x))
+    other_plane = pick(first, jnp.logical_not(flat), flat | root)
+    parent_a = pick(other_plane, pick(first, chain_a, stem), in_a)
+    parent_b = pick(other_plane, pick(first, chain_b, stem), in_b)
+    beyond = z >= 5
+    turn = pick(flat | (z == 4), 2, pick(beyond, 1, 0))
+    side = (yh == 1) & (x == 3) & jnp.logical_not(flat)
+    order = pick(first, pick(twin, turn, pick(x == 3, 1, 0)), pick(side, 2, 0))
+    passes = (flat & root) | (twin & flat)
+    return kids, parent_a, parent_b, order, passes
+
+
+def start_time(core, yh, z, x):
+    first = core == 0
+    dz = jnp.minimum(z, NZ - z)
+    flat = z == 0
+    root = (yh == 0) & (x == 0)
+    dx = pick(x % 2 == 1, 1, pick(root & (jnp.logical_not(first) | flat), 0, 2))
+    dz = dz + pick(flat & jnp.logical_not(first) & jnp.logical_not(root), 2, 0)
+    return (pick(first, 7, 5) * dx + pick(first, 6, 4) * dz + pick(first, 8, 6) * yh) * (CHUNKS // 32)
 
 
 def place():
     r = lax.axis_index("row")
     c = lax.axis_index("col")
     return r, c, r % 2, r // 2, c // (NX * NZ), (c // NX) % NZ, c % NX
-
-
-def hops(core, yh, z, x):
-    dz = jnp.minimum(z, NZ - z)
-    dx = jnp.minimum(x, NX - x)
-    root = (yh == 0) & (x == 0)
-    flat = z == 0
-    around = pick(core == 0, root & jnp.logical_not(flat), flat & jnp.logical_not(root))
-    return dz + dx + yh + pick(around, 2, 0)
 
 
 def local_row(p, nb, row_count):
@@ -94,7 +113,7 @@
     far = (1 - yl) * 2 + core
     source = c == 0
     other = jnp.logical_not(source)
-    kids, parent = tree(core, yh, z, x)
+    kids, parent_a, parent_b, order, passes = tree(core, yh, z, x)
     rows, cols = mat_hbm.shape
     tile = rows // TILES
     chunk = rows // CHUNKS
@@ -108,22 +127,36 @@
         at = pl.ds(pl.multiple_of(t * tile, tile), tile)
         return pltpu.make_async_copy(mat_hbm.at[at], mat.at[at], in_sem.at[t])
 
-    def forward(j, k):
-        at = pl.ds(pl.multiple_of(j * chunk, chunk), chunk)
+    split_point = CHUNKS // 2
+
+    def turn(mode, j):
+        late_first = pick(j < split_point, j + split_point, j - split_point)
+        return pick(mode == 0, j, pick(mode == 1, late_first, j // 2 + (j % 2) * split_point))
+
+    def forward(i, k):
+        at = pl.ds(pl.multiple_of(i * chunk, chunk), chunk)
         return pltpu.make_async_remote_copy(
             src_ref=panel.at[at],
             dst_ref=panel.at[at],
             send_sem=send_sem.at[k],
-            recv_sem=recv_sem.at[j],
-            device_id={"row": r, "col": kids[k][1]},
+            recv_sem=recv_sem.at[i],
+            device_id={"row": r, "col": kids[k][2]},
             device_id_type=pl.DeviceIdType.MESH,
         )
 
-    def send(j):
-        for k in range(SLOTS):
-            @pl.when(kids[k][0])
+    def send(i, second=False):
+        head = i < split_point
+        for k, (valid, kind, _) in enumerate(kids):
+            match = jnp.logical_xor((kind % 2) == 1, head)
+            both = kind < 2
+            if second:
+                go = both & jnp.logical_not(match)
+            else:
+                go = match | (both & jnp.logical_not(passes))
+
+            @pl.when(valid & go)
             def _():
-                forward(j, k).start()
+                forward(i, k).start()
 
     def swap(step, src, dst, to):
         return pltpu.make_async_remote_copy(
@@ -145,7 +178,11 @@
 
     @pl.when(other)
     def _():
-        signal(r, parent)
+        signal(r, parent_a)
+
+        @pl.when(parent_b != parent_a)
+        def _():
+            signal(r, parent_b)
 
     signal(pair, c)
     signal(far, c)
@@ -177,13 +214,20 @@
 
     @pl.when(source)
     def _():
-        @pl.loop(0, TILES)
+        @pl.loop(0, TILES // 2)
         def _(t):
-            load(t).wait()
-            at = pl.ds(pl.multiple_of(t * tile, tile), tile)
-            panel[at] = mat[at, :width].astype(panel.dtype)
-            for s in range(per):
-                send(t * per + s)
+            for half_t in (t, t + TILES // 2):
+                load(half_t).wait()
+                at = pl.ds(pl.multiple_of(half_t * tile, tile), tile)
+                panel[at] = mat[at, :width].astype(panel.dtype)
+
+            @pl.loop(t * 2 * per, (t + 1) * 2 * per)
+            def _(j):
+                send(turn(2, j))
+
+        @pl.loop(0, CHUNKS)
+        def _(j):
+            send(turn(2, j), second=True)
 
     @pl.when(other)
     def _():
@@ -201,6 +245,18 @@
             out[pl.ds(s, 1)] = got[s]
 
     with_pair.start()
+
+    def sent():
+        for k, (valid, kind, col) in enumerate(kids):
+            for whole in (True, False):
+                part = panel if whole else panel.at[pl.ds(0, rows // 2)]
+
+                @pl.when(valid & ((kind < 2) == whole))
+                def _():
+                    pltpu.make_async_remote_copy(
+                        src_ref=part, dst_ref=part, send_sem=send_sem.at[k], recv_sem=recv_sem.at[0],
+                        device_id={"row": r, "col": col}, device_id_type=pl.DeviceIdType.MESH,
+                    ).wait_send()
 
     def step_across():
         with_pair.wait_recv()
@@ -272,19 +328,20 @@
                 panel[at], u_half[:, width:], preferred_element_type=jnp.float32
             )
 
-    depth = hops(core, yh, z, x)
-    scale = CHUNKS // 8
-    gap = (scale * 3) // 2
-    late = (yh == 1) & (x == 0) & (z == 0)
+    came = start_time(core, yh, z, x)
+    late = (yh == 0) & (z == 0) & (x % 2 == 1)
     compact = (expect == 2) & jnp.logical_not(late)
     spread_out = jnp.logical_not(compact)
-    late_go = pick(core == 0, CHUNKS - scale // 2, scale * 5)
-    at_across = pick(late, late_go, pick((depth <= 1) & other, scale, 0))
-    at_pass = pick(late, pick(core == 0, CHUNKS, late_go + 1), jnp.maximum(0, gap * (5 - depth) + 1))
-    at_u = pick(late, at_pass + 1, pick(depth >= 6, 0, gap * (6 - depth) + 1))
-    at_across = pick(source, 0, at_across)
-    at_pass = pick(source, 1, at_pass)
-    at_u = pick(source, 2, at_u)
+    unit = CHUNKS // 32
+    free_link = unit * 23
+    swap_time = pick(late, free_link, unit * 11)
+    at_across = jnp.maximum(0, swap_time - came)
+    at_pass = jnp.maximum(0, pick(late, free_link + unit * 23, unit * 33) - came)
+    last = pick(passes, 2 * CHUNKS, CHUNKS)
+    settle = passes & other
+    at_across = pick(source, 0, pick(settle, jnp.minimum(2 * at_across, last), at_across))
+    at_pass = pick(source, 1, pick(settle, last, at_pass))
+    at_u = pick(source, 2, pick(settle, last + 1, at_pass + unit * 6))
     split_at = 4 * SIDES
     swap_at = split_at + 2 * SIDES
     steps = swap_at + 2 * TILES
@@ -304,37 +361,50 @@
         def _(t):
             step_swap(t)
 
-    @pl.loop(0, pick(compact, CHUNKS, jnp.maximum(CHUNKS, at_u + steps)))
-    def _(j):
-        pl.when(spread_out & (j == at_across))(step_across)
-        pl.when(spread_out & (j == at_pass))(step_pass)
-
-        @pl.when((j < CHUNKS) & other)
-        def _():
-            forward(j, 0).wait_recv()
-            send(j)
-
-        @pl.when(compact)
-        def _():
-            update(j, chunk)
-
-        q = j - at_u
-        pl.when(spread_out & (q == 0))(step_wait)
-
-        @pl.when(spread_out & (q >= 0) & (q < split_at) & (q % 4 == 0))
-        def _():
-            step_u(q // 4)
-
-        @pl.when(spread_out & (q >= split_at) & (q < swap_at) & (q % 2 == 0))
-        def _():
-            step_split((q - split_at) // 2)
-
-        @pl.when(spread_out & (q >= swap_at) & (q < steps) & (q % 2 == 0))
-        def _():
-            step_swap((q - swap_at) // 2)
+        group = CHUNKS // 4
+
+        @pl.loop(0, 4)
+        def _(g):
+            @pl.loop(g * group, (g + 1) * group)
+            def _(j):
+                forward(turn(order, j), 0).wait_recv()
+
+            one = pick(order == 0, 2 * g, pick(order == 1, (2 * g + TILES // 2) % TILES, g))
+            update(one, tile)
+            update(one + pick(order == 2, TILES // 2, 1), tile)
 
     @pl.when(spread_out)
     def _():
+        @pl.loop(0, jnp.maximum(last, at_u + steps))
+        def _(j):
+            pl.when(j == at_across)(step_across)
+            pl.when(j == at_pass)(step_pass)
+
+            @pl.when((j < CHUNKS) & other)
+            def _():
+                i = turn(order, j)
+                forward(i, 0).wait_recv()
+                send(i)
+
+            @pl.when(settle & (j >= CHUNKS) & (j < last))
+            def _():
+                send(turn(2, jnp.minimum(j - CHUNKS, CHUNKS - 1)), second=True)
+
+            q = j - at_u
+            pl.when(q == 0)(step_wait)
+
+            @pl.when((q >= 0) & (q < split_at) & (q % 4 == 0))
+            def _():
+                step_u(q // 4)
+
+            @pl.when((q >= split_at) & (q < swap_at) & (q % 2 == 0))
+            def _():
+                step_split((q - split_at) // 2)
+
+            @pl.when((q >= swap_at) & (q < steps) & (q % 2 == 0))
+            def _():
+                step_swap((q - swap_at) // 2)
+
         @pl.loop(0, TILES)
         def _(t):
             update(t, tile)
@@ -342,13 +412,7 @@
     with_pair.wait_send()
     across.wait_send()
     pass_on.wait_send()
-    for k in range(SLOTS):
-        @pl.when(kids[k][0])
-        def _():
-            pltpu.make_async_remote_copy(
-                src_ref=panel, dst_ref=panel, send_sem=send_sem.at[k], recv_sem=recv_sem.at[0],
-                device_id={"row": r, "col": kids[k][1]}, device_id_type=pl.DeviceIdType.MESH,
-            ).wait_send()
+    sent()
 
 
 def finish_kernel(mat, u_ref, takes, out, u_out, moved_out, moved, takes_at, sem):

time: 41.2 us -> 40.3 us (0.978)
  the two profiles are of different devices: /device:TPU:16 before, /device:TPU:155 now
where the time goes in v7:
time: 40.3 us; the launch traced here: 40.2 us
  Pallas kernels  39.6 us (98%)
  between operations  0.64 us (2%)
    pallas_call x1, Pallas kernels, body(): pl.pallas_call(move_kernel, out_shape=(shape((rows + 8, cols), f32), shap...  37.2 us
    pallas_call x1, Pallas kernels, body(): pl.pallas_call(finish_kernel, out_shape=(shape((rows, cols), f32), shape(...  2.43 us

profile of v7, /device:TPU:155, one launch (start us, length us, event | category | flops | bytes accessed | tf_op | source)
XLA Modules:
  0.0 40.2 jit_solution(10971097398779838391)
XLA Ops:
  0.6 37.2 %move.1 = (f32[2056,512]{1,0:T(8,128)S(1)}, f32[256,512]{1,0:T(8,128)S(1)}, s32[1,256]{1,0:T(1,128)S(1)}) custom-call(s32[1,256]{1,0:T(1,128)} %bitcast.1, f32[2048,512]{1,0:T(8,128)} %mat_hbm.1, f32[256,256]{1,0:T(8,128)} %l_hbm.1), custom_call_target="tpu_custom_call" | custom-call | tf_op jit(solution)/shard_map/move/pallas_call | solution.py:455
  37.8 2.4 %finish.1 = (f32[2048,512]{1,0:T(8,128)}, f32[256,512]{1,0:T(8,128)}, f32[256,512]{1,0:T(8,128)}) custom-call(f32[2056,512]{1,0:T(8,128)S(1)} %get-tuple-element.6.mat, f32[256,512]{1,0:T(8,128)S(1)} %get-tuple-element.7.u_ref, s32[1,256]{1,0:T(1,128)S(1)} %get-tuple-element.8.takes), custom_call_target="tpu_custom_call" | custom-call | tf_op jit(solution)/shard_map/finish/pallas_call | solution.py:484

commit v8 on v7

--- a/solution.py
+++ b/solution.py
@@ -34,6 +34,8 @@
     down = (z == 6) | (z == 7)
     odd = (x % 2) == 1
     inplane = pick(first, flat, jnp.logical_not(flat))
+    folded = inplane & (first | (z == 1) | (z == 7))
+    plain = inplane & jnp.logical_not(folded)
     twin = first & ((x == 2) | ((yh == 1) & (x == 0)))
     only = pick(x == 1, 2, 3)
     along = pick(first, off, root)
@@ -41,17 +43,18 @@
     k0 = column(yh, pick(flat, 1, pick(up, z + 1, z - 1)), x)
     c0 = pick(twin & (z == 3), 2, pick(twin & (z == 5), 3, 0))
     drop = second & (z == 1) & off
-    v2 = (along & flat) | drop
-    k2 = column(yh, pick(drop, 0, 7), x)
+    over = plain & root
+    v2 = (along & flat) | drop | over
+    k2 = pick(over, column(1, z, 0), column(yh, pick(drop, 0, 7), x))
     c2 = pick(twin, 1, 0)
     back = first & jnp.logical_not(flat) & (yh == 0) & (x == 1)
-    v1 = (inplane & jnp.logical_not((yh == 0) & (x == 2))) | back
+    v1 = (folded & jnp.logical_not((yh == 0) & (x == 2))) | back | (plain & (x <= 1))
     x1 = pick(odd, 2, pick(x == 2, 1, pick(yh == 0, 1, 3)))
-    k1 = column(yh, z, pick(back, 0, x1))
-    c1 = pick(back | root, 0, pick(odd, only, pick(x == 2, 3, 2)))
-    v3 = inplane & (root | odd)
-    k3 = pick(root, column(0, z, 3), pick(yh == 0, column(1, z, x), column(1, z, 0)))
-    c3 = pick(root, pick(first, 1, 0), only)
+    k1 = column(yh, z, pick(back, 0, pick(plain, x + 1, x1)))
+    c1 = pick(back | root | plain, 0, pick(odd, only, pick(x == 2, 3, 2)))
+    v3 = (folded & (root | odd)) | (plain & (x == 0))
+    k3 = pick(root | plain, column(yh, z, 3), pick(yh == 0, column(1, z, x), column(1, z, 0)))
+    c3 = pick(root | plain, pick(first, 1, 0), only)
     kids = ((v0, c0, k0), (v1, c1, k1), (v2, c2, k2), (v3, c3, k3))
     near = pick(z <= 4, z - 1, (z + 1) % NZ)
     in_a = pick(
@@ -68,11 +71,12 @@
     chain_b = pick(twin & (z == 4), column(yh, 5, x), chain_a)
     stem = pick(root, column(0, near, 0), column(yh, 1, x))
     other_plane = pick(first, jnp.logical_not(flat), flat | root)
-    parent_a = pick(other_plane, pick(first, chain_a, stem), in_a)
-    parent_b = pick(other_plane, pick(first, chain_b, stem), in_b)
+    in_plain = pick(x == 2, column(yh, z, 1), pick(x == 0, column(0, z, 0), column(yh, z, 0)))
+    parent_a = pick(other_plane, pick(first, chain_a, stem), pick(plain, in_plain, in_a))
+    parent_b = pick(other_plane, pick(first, chain_b, stem), pick(plain, in_plain, in_b))
     beyond = z >= 5
     turn = pick(flat | (z == 4), 2, pick(beyond, 1, 0))
-    side = (yh == 1) & (x == 3) & jnp.logical_not(flat)
+    side = (yh == 1) & (x == 3) & folded
     order = pick(first, pick(twin, turn, pick(x == 3, 1, 0)), pick(side, 2, 0))
     passes = (flat & root) | (twin & flat)
     return kids, parent_a, parent_b, order, passes
@@ -83,7 +87,9 @@
     dz = jnp.minimum(z, NZ - z)
     flat = z == 0
     root = (yh == 0) & (x == 0)
-    dx = pick(x % 2 == 1, 1, pick(root & (jnp.logical_not(first) | flat), 0, 2))
+    straight = (z != 0) & (z != 1) & (z != 7) & (x == 0)
+    none = (root & (jnp.logical_not(first) | flat)) | (jnp.logical_not(first) & straight)
+    dx = pick(x % 2 == 1, 1, pick(none, 0, 2))
     dz = dz + pick(flat & jnp.logical_not(first) & jnp.logical_not(root), 2, 0)
     return (pick(first, 7, 5) * dx + pick(first, 6, 4) * dz + pick(first, 8, 6) * yh) * (CHUNKS // 32)
 
@@ -329,22 +335,38 @@
             )
 
     came = start_time(core, yh, z, x)
-    late = (yh == 0) & (z == 0) & (x % 2 == 1)
+    edge = (z == 1) | (z == 7)
+    late = (yh == 0) & (((z == 0) & (x % 2 == 1)) | (edge & (x == 1)))
     compact = (expect == 2) & jnp.logical_not(late)
     spread_out = jnp.logical_not(compact)
     unit = CHUNKS // 32
-    free_link = unit * 23
+    free_link = unit * 25
     swap_time = pick(late, free_link, unit * 11)
     at_across = jnp.maximum(0, swap_time - came)
     at_pass = jnp.maximum(0, pick(late, free_link + unit * 23, unit * 33) - came)
+    slow = (core == 1) & (yh == 1) & (z != 0) & jnp.logical_not(edge)
+    at_pass = pick(slow, at_pass // 2, at_pass)
+    lags = (core == 1) & (yh == 1) & edge & (x % 2 == 1)
+    at_pass = pick(lags, pick(x == 1, CHUNKS // 2 - 1, CHUNKS // 8), at_pass)
+    after_pass = jnp.maximum(0, unit * 41 - came)
+    after_pass = pick(slow, after_pass * 2 // 3, after_pass)
+    after_pass = pick(lags & (x == 1), CHUNKS // 2, jnp.maximum(after_pass, at_pass + 1))
     last = pick(passes, 2 * CHUNKS, CHUNKS)
     settle = passes & other
     at_across = pick(source, 0, pick(settle, jnp.minimum(2 * at_across, last), at_across))
     at_pass = pick(source, 1, pick(settle, last, at_pass))
-    at_u = pick(source, 2, pick(settle, last + 1, at_pass + unit * 6))
+    at_u = pick(source, 2, pick(settle, last + 1, pick(late, at_pass + unit * 8, after_pass)))
     split_at = 4 * SIDES
     swap_at = split_at + 2 * SIDES
     steps = swap_at + 2 * TILES
+
+    def tile_turn(p):
+        upper = TILES // 2
+        return pick(order == 0, p, pick(order == 1, (p + upper) % TILES, p // 2 + (p % 2) * upper))
+
+    def early(p):
+        done = pick(order == 2, (p // 2 + 1) * 2 * per - 1, (p + 1) * per - 1)
+        return at_u + swap_at + 2 * p + 1 >= jnp.minimum(done, CHUNKS - 1)
 
     @pl.when(compact)
     def _():
@@ -403,11 +425,19 @@
 
             @pl.when((q >= swap_at) & (q < steps) & (q % 2 == 0))
             def _():
-                step_swap((q - swap_at) // 2)
+                step_swap(tile_turn((q - swap_at) // 2))
+
+            p = (q - swap_at) // 2
+
+            @pl.when((q >= swap_at) & (q < steps) & (q % 2 == 1) & early(p))
+            def _():
+                update(tile_turn(p), tile)
 
         @pl.loop(0, TILES)
-        def _(t):
-            update(t, tile)
+        def _(p):
+            @pl.when(jnp.logical_not(early(p)))
+            def _():
+                update(tile_turn(p), tile)
 
     with_pair.wait_send()
     across.wait_send()

time: 40.3 us -> 36.4 us (0.903)
  the two profiles are of different devices: /device:TPU:155 before, /device:TPU:120 now
where the time goes in v8:
time: 36.4 us; the launch traced here: 36.3 us
  Pallas kernels  35.6 us (98%)
  between operations  0.64 us (2%)
    pallas_call x1, Pallas kernels, body(): pl.pallas_call(move_kernel, out_shape=(shape((rows + 8, cols), f32), shap...  33.2 us
    pallas_call x1, Pallas kernels, body(): pl.pallas_call(finish_kernel, out_shape=(shape((rows, cols), f32), shape(...  2.43 us

profile of v8, /device:TPU:120, one launch (start us, length us, event | category | flops | bytes accessed | tf_op | source)
XLA Modules:
  0.0 36.3 jit_solution(4898257160827333837)
XLA Ops:
  0.6 33.2 %move.1 = (f32[2056,512]{1,0:T(8,128)S(1)}, f32[256,512]{1,0:T(8,128)S(1)}, s32[1,256]{1,0:T(1,128)S(1)}) custom-call(s32[1,256]{1,0:T(1,128)} %bitcast.1, f32[2048,512]{1,0:T(8,128)} %mat_hbm.1, f32[256,256]{1,0:T(8,128)} %l_hbm.1), custom_call_target="tpu_custom_call" | custom-call | tf_op jit(solution)/shard_map/move/pallas_call | solution.py:485
  33.8 2.4 %finish.1 = (f32[2048,512]{1,0:T(8,128)}, f32[256,512]{1,0:T(8,128)}, f32[256,512]{1,0:T(8,128)}) custom-call(f32[2056,512]{1,0:T(8,128)S(1)} %get-tuple-element.6.mat, f32[256,512]{1,0:T(8,128)S(1)} %get-tuple-element.7.u_ref, s32[1,256]{1,0:T(1,128)S(1)} %get-tuple-element.8.takes), custom_call_target="tpu_custom_call" | custom-call | tf_op jit(solution)/shard_map/finish/pallas_call | solution.py:514

commit v9 on v8

--- a/solution.py
+++ b/solution.py
@@ -75,7 +75,7 @@
     parent_a = pick(other_plane, pick(first, chain_a, stem), pick(plain, in_plain, in_a))
     parent_b = pick(other_plane, pick(first, chain_b, stem), pick(plain, in_plain, in_b))
     beyond = z >= 5
-    turn = pick(flat | (z == 4), 2, pick(beyond, 1, 0))
+    turn = pick(flat | (z == 4), pick(flat & (x == 0), 3, 2), pick(beyond, 1, 0))
     side = (yh == 1) & (x == 3) & folded
     order = pick(first, pick(twin, turn, pick(x == 3, 1, 0)), pick(side, 2, 0))
     passes = (flat & root) | (twin & flat)
@@ -137,7 +137,12 @@
 
     def turn(mode, j):
         late_first = pick(j < split_point, j + split_point, j - split_point)
-        return pick(mode == 0, j, pick(mode == 1, late_first, j // 2 + (j % 2) * split_point))
+        even = j // 2 + (j % 2) * split_point
+        lead = CHUNKS // 8
+        m = jnp.maximum(j - lead, 0)
+        led = pick(m % 2 == 0, m // 2 + split_point, m // 2 + lead)
+        led = pick(j < lead, j, pick(j < CHUNKS - lead, led, j))
+        return pick(mode == 0, j, pick(mode == 1, late_first, pick(mode == 2, even, led)))
 
     def forward(i, k):
         at = pl.ds(pl.multiple_of(i * chunk, chunk), chunk)
@@ -180,6 +185,17 @@
     across = swap(1, comb, m_far.at[mine], far)
     pass_on = swap(2, m_far.at[mine], m_far.at[mine], pair)
 
+    load_p = pltpu.make_async_copy(row_hbm, pivot_row, in_sem.at[TILES])
+    give_p = pltpu.make_async_copy(from_row, from_at, in_sem.at[TILES + 1])
+    load_l = pltpu.make_async_copy(l_hbm, l_inverse, in_sem.at[TILES + 2])
+    load(0).start()
+    load(TILES // 2).start()
+    load_p.start()
+    for t in range(1, TILES):
+        if t != TILES // 2:
+            load(t).start()
+    load_l.start()
+
     barrier = pltpu.get_barrier_semaphore()
 
     @pl.when(other)
@@ -192,26 +208,20 @@
 
     signal(pair, c)
     signal(far, c)
-    load_p = pltpu.make_async_copy(row_hbm, pivot_row, in_sem.at[TILES])
-    give_p = pltpu.make_async_copy(from_row, from_at, in_sem.at[TILES + 1])
-    load_l = pltpu.make_async_copy(l_hbm, l_inverse, in_sem.at[TILES + 2])
-    load_p.start()
-    load(0).start()
-    for t in range(1, TILES):
-        load(t).start()
-    load_l.start()
-
-    load_p.wait()
-    owner, local = local_row(pivot_row[...], nb, row_count)
-    from_row[...] = jnp.where(owner == r, local, lax.broadcasted_iota(jnp.int32, (1, nb), 1))
-    takes[...] = jnp.where((owner == r) & (pivot_row[...] >= nb), local, rows)
-    mat[pl.ds(rows, 8)] = jnp.zeros((8, cols), mat.dtype)
-    kind = jnp.where(owner == r, 0.0, jnp.where(owner == pair, 1.0, 2.0))
-    down = lax.broadcasted_iota(jnp.int32, (nb, nb), 0)
-    along = lax.broadcasted_iota(jnp.int32, (nb, nb), 1)
-    spread = jnp.where(down == along, jnp.broadcast_to(kind, (nb, nb)), 0.0)
-    code[...] = jnp.sum(spread, axis=1, keepdims=True)
-    give_p.start()
+    def prepare():
+        load_p.wait()
+        owner, local = local_row(pivot_row[...], nb, row_count)
+        from_row[...] = jnp.where(owner == r, local, lax.broadcasted_iota(jnp.int32, (1, nb), 1))
+        takes[...] = jnp.where((owner == r) & (pivot_row[...] >= nb), local, rows)
+        mat[pl.ds(rows, 8)] = jnp.zeros((8, cols), mat.dtype)
+        kind = jnp.where(owner == r, 0.0, jnp.where(owner == pair, 1.0, 2.0))
+        down = lax.broadcasted_iota(jnp.int32, (nb, nb), 0)
+        along = lax.broadcasted_iota(jnp.int32, (nb, nb), 1)
+        spread = jnp.where(down == along, jnp.broadcast_to(kind, (nb, nb)), 0.0)
+        code[...] = jnp.sum(spread, axis=1, keepdims=True)
+        give_p.start()
+
+    pl.when(other)(prepare)
 
     expect = 2
     for k in range(SLOTS):
@@ -234,6 +244,8 @@
         @pl.loop(0, CHUNKS)
         def _(j):
             send(turn(2, j), second=True)
+
+        prepare()
 
     @pl.when(other)
     def _():
@@ -347,6 +359,7 @@
     slow = (core == 1) & (yh == 1) & (z != 0) & jnp.logical_not(edge)
     at_pass = pick(slow, at_pass // 2, at_pass)
     lags = (core == 1) & (yh == 1) & edge & (x % 2 == 1)
+    fast = lags & (z == 7)
     at_pass = pick(lags, pick(x == 1, CHUNKS // 2 - 1, CHUNKS // 8), at_pass)
     after_pass = jnp.maximum(0, unit * 41 - came)
     after_pass = pick(slow, after_pass * 2 // 3, after_pass)
@@ -366,7 +379,8 @@
 
     def early(p):
         done = pick(order == 2, (p // 2 + 1) * 2 * per - 1, (p + 1) * per - 1)
-        return at_u + swap_at + 2 * p + 1 >= jnp.minimum(done, CHUNKS - 1)
+        step = swap_at + 2 * p
+        return at_u + pick(fast, step // 2, step) >= jnp.minimum(done, CHUNKS - 1)
 
     @pl.when(compact)
     def _():
@@ -397,7 +411,7 @@
 
     @pl.when(spread_out)
     def _():
-        @pl.loop(0, jnp.maximum(last, at_u + steps))
+        @pl.loop(0, jnp.maximum(last, at_u + pick(fast, steps // 2, steps)))
         def _(j):
             pl.when(j == at_across)(step_across)
             pl.when(j == at_pass)(step_pass)
@@ -412,7 +426,7 @@
             def _():
                 send(turn(2, jnp.minimum(j - CHUNKS, CHUNKS - 1)), second=True)
 
-            q = j - at_u
+            q = (j - at_u) * pick(fast, 2, 1)
             pl.when(q == 0)(step_wait)
 
             @pl.when((q >= 0) & (q < split_at) & (q % 4 == 0))
@@ -425,13 +439,12 @@
 
             @pl.when((q >= swap_at) & (q < steps) & (q % 2 == 0))
             def _():
-                step_swap(tile_turn((q - swap_at) // 2))
-
-            p = (q - swap_at) // 2
-
-            @pl.when((q >= swap_at) & (q < steps) & (q % 2 == 1) & early(p))
-            def _():
-                update(tile_turn(p), tile)
+                p = (q - swap_at) // 2
+                step_swap(tile_turn(p))
+
+                @pl.when(early(p))
+                def _():
+                    update(tile_turn(p), tile)
 
         @pl.loop(0, TILES)
         def _(p):
@@ -460,16 +473,19 @@
         copy.start()
     give_t.wait()
 
-    @pl.loop(0, nb // 8)
-    def _(g):
+    def gather(g):
         eight = moved.at[pl.ds(pl.multiple_of(g * 8, 8), 8)]
         got = [mat[pl.ds(takes_at[0, g * 8 + s], 1)] for s in range(8)]
         for s in range(8):
             eight[pl.ds(s, 1)] = got[s]
 
-    last = pltpu.make_async_copy(moved, moved_out, sem.at[TILES + 2])
-    last.start()
-    copies.append(last)
+    part = nb // 4
+    for p in range(4):
+        pl.loop(p * part // 8, (p + 1) * part // 8)(gather)
+        at = pl.ds(p * part, part)
+        last = pltpu.make_async_copy(moved.at[at], moved_out.at[at], sem.at[TILES + 2 + p])
+        last.start()
+        copies.append(last)
     for copy in copies:
         copy.wait()
 
@@ -519,7 +535,7 @@
         scratch_shapes=[
             pltpu.VMEM((nb, cols), f32),
             pltpu.SMEM((1, nb), i32),
-            pltpu.SemaphoreType.DMA((TILES + 3,)),
+            pltpu.SemaphoreType.DMA((TILES + 6,)),
         ],
         compiler_params=pltpu.CompilerParams(vmem_limit_bytes=FINISH_VMEM),
         name="finish",

time: 36.4 us -> 36.5 us (level)
  no operation moved by 1% of the time
where the time goes in v9:
time: 36.5 us; the launch traced here: 36.4 us
  Pallas kernels  35.7 us (98%)
  between operations  0.64 us (2%)
    pallas_call x1, Pallas kernels, body(): pl.pallas_call(move_kernel, out_shape=(shape((rows + 8, cols), f32), shap...  33.3 us
    pallas_call x1, Pallas kernels, body(): pl.pallas_call(finish_kernel, out_shape=(shape((rows, cols), f32), shape(...  2.43 us

profile of v9, /device:TPU:120, one launch (start us, length us, event | category | flops | bytes accessed | tf_op | source)
XLA Modules:
  0.0 36.4 jit_solution(6658505812728119894)
XLA Ops:
  0.6 33.3 %move.1 = (f32[2056,512]{1,0:T(8,128)S(1)}, f32[256,512]{1,0:T(8,128)S(1)}, s32[1,256]{1,0:T(1,128)S(1)}) custom-call(s32[1,256]{1,0:T(1,128)} %bitcast.1, f32[2048,512]{1,0:T(8,128)} %mat_hbm.1, f32[256,256]{1,0:T(8,128)} %l_hbm.1), custom_call_target="tpu_custom_call" | custom-call | tf_op jit(solution)/shard_map/move/pallas_call | solution.py:501
  33.9 2.4 %finish.1 = (f32[2048,512]{1,0:T(8,128)}, f32[256,512]{1,0:T(8,128)}, f32[256,512]{1,0:T(8,128)}) custom-call(f32[2056,512]{1,0:T(8,128)S(1)} %get-tuple-element.6.mat, f32[256,512]{1,0:T(8,128)S(1)} %get-tuple-element.7.u_ref, s32[1,256]{1,0:T(1,128)S(1)} %get-tuple-element.8.takes), custom_call_target="tpu_custom_call" | custom-call | tf_op jit(solution)/shard_map/finish/pallas_call | solution.py:530

commit v10 on v9

--- a/solution.py
+++ b/solution.py
@@ -359,9 +359,9 @@
     slow = (core == 1) & (yh == 1) & (z != 0) & jnp.logical_not(edge)
     at_pass = pick(slow, at_pass // 2, at_pass)
     lags = (core == 1) & (yh == 1) & edge & (x % 2 == 1)
-    fast = lags & (z == 7)
+    fast = (lags & (z == 7)) | ((core == 1) & (yh == 1) & (z == 1) & (x == 0))
     at_pass = pick(lags, pick(x == 1, CHUNKS // 2 - 1, CHUNKS // 8), at_pass)
-    after_pass = jnp.maximum(0, unit * 41 - came)
+    after_pass = jnp.maximum(unit * 3, unit * 41 - came)
     after_pass = pick(slow, after_pass * 2 // 3, after_pass)
     after_pass = pick(lags & (x == 1), CHUNKS // 2, jnp.maximum(after_pass, at_pass + 1))
     last = pick(passes, 2 * CHUNKS, CHUNKS)

time: 36.5 us -> 36.2 us (level)
  no operation moved by 1% of the time
where the time goes in v10:
time: 36.2 us; the launch traced here: 36.1 us
  Pallas kernels  35.5 us (98%)
  between operations  0.64 us (2%)
    pallas_call x1, Pallas kernels, body(): pl.pallas_call(move_kernel, out_shape=(shape((rows + 8, cols), f32), shap...  33 us
    pallas_call x1, Pallas kernels, body(): pl.pallas_call(finish_kernel, out_shape=(shape((rows, cols), f32), shape(...  2.43 us

profile of v10, /device:TPU:120, one launch (start us, length us, event | category | flops | bytes accessed | tf_op | source)
XLA Modules:
  0.0 36.1 jit_solution(987287524849970166)
XLA Ops:
  0.6 33.0 %move.1 = (f32[2056,512]{1,0:T(8,128)S(1)}, f32[256,512]{1,0:T(8,128)S(1)}, s32[1,256]{1,0:T(1,128)S(1)}) custom-call(s32[1,256]{1,0:T(1,128)} %bitcast.1, f32[2048,512]{1,0:T(8,128)} %mat_hbm.1, f32[256,256]{1,0:T(8,128)} %l_hbm.1), custom_call_target="tpu_custom_call" | custom-call | tf_op jit(solution)/shard_map/move/pallas_call | solution.py:501
  33.7 2.4 %finish.1 = (f32[2048,512]{1,0:T(8,128)}, f32[256,512]{1,0:T(8,128)}, f32[256,512]{1,0:T(8,128)}) custom-call(f32[2056,512]{1,0:T(8,128)S(1)} %get-tuple-element.6.mat, f32[256,512]{1,0:T(8,128)S(1)} %get-tuple-element.7.u_ref, s32[1,256]{1,0:T(1,128)S(1)} %get-tuple-element.8.takes), custom_call_target="tpu_custom_call" | custom-call | tf_op jit(solution)/shard_map/finish/pallas_call | solution.py:530

commit v11 on v10

--- a/solution.py
+++ b/solution.py
@@ -191,10 +191,14 @@
     load(0).start()
     load(TILES // 2).start()
     load_p.start()
-    for t in range(1, TILES):
-        if t != TILES // 2:
-            load(t).start()
-    load_l.start()
+
+    def load_rest():
+        for t in range(1, TILES):
+            if t != TILES // 2:
+                load(t).start()
+        load_l.start()
+
+    pl.when(other)(load_rest)
 
     barrier = pltpu.get_barrier_semaphore()
 
@@ -232,14 +236,23 @@
     def _():
         @pl.loop(0, TILES // 2)
         def _(t):
-            for half_t in (t, t + TILES // 2):
-                load(half_t).wait()
-                at = pl.ds(pl.multiple_of(half_t * tile, tile), tile)
-                panel[at] = mat[at, :width].astype(panel.dtype)
-
-            @pl.loop(t * 2 * per, (t + 1) * 2 * per)
-            def _(j):
-                send(turn(2, j))
+            load(t).wait()
+            load(t + TILES // 2).wait()
+            pl.when(t == 0)(load_rest)
+
+            @pl.loop(t * per, (t + 1) * per)
+            def _(i):
+                for piece in (i, i + split_point):
+                    at = pl.ds(pl.multiple_of(piece * chunk, chunk), chunk)
+                    panel[at] = mat[at, :width].astype(panel.dtype)
+
+                @pl.when(i > 0)
+                def _():
+                    send(jnp.maximum(i - 1, 0))
+                    send(jnp.maximum(i - 1, 0) + split_point)
+
+        send(split_point - 1)
+        send(CHUNKS - 1)
 
         @pl.loop(0, CHUNKS)
         def _(j):

time: 36.2 us -> 36.6 us (1.011); the launches traced: 36.1 us -> 36.1 us
  no operation moved by 1% of the time
where the time goes in v11:
time: 36.6 us; the launch traced here: 36.1 us
  Pallas kernels  35.4 us (97%)
  between operations  0.64 us (2%)
    pallas_call x1, Pallas kernels, body(): pl.pallas_call(move_kernel, out_shape=(shape((rows + 8, cols), f32), shap...  33 us
    pallas_call x1, Pallas kernels, body(): pl.pallas_call(finish_kernel, out_shape=(shape((rows, cols), f32), shape(...  2.43 us

profile of v11, /device:TPU:120, one launch (start us, length us, event | category | flops | bytes accessed | tf_op | source)
XLA Modules:
  0.0 36.1 jit_solution(11889333362033112360)
XLA Ops:
  0.6 33.0 %move.1 = (f32[2056,512]{1,0:T(8,128)S(1)}, f32[256,512]{1,0:T(8,128)S(1)}, s32[1,256]{1,0:T(1,128)S(1)}) custom-call(s32[1,256]{1,0:T(1,128)} %bitcast.1, f32[2048,512]{1,0:T(8,128)} %mat_hbm.1, f32[256,256]{1,0:T(8,128)} %l_hbm.1), custom_call_target="tpu_custom_call" | custom-call | tf_op jit(solution)/shard_map/move/pallas_call | solution.py:514
  33.7 2.4 %finish.1 = (f32[2048,512]{1,0:T(8,128)}, f32[256,512]{1,0:T(8,128)}, f32[256,512]{1,0:T(8,128)}) custom-call(f32[2056,512]{1,0:T(8,128)S(1)} %get-tuple-element.6.mat, f32[256,512]{1,0:T(8,128)S(1)} %get-tuple-element.7.u_ref, s32[1,256]{1,0:T(1,128)S(1)} %get-tuple-element.8.takes), custom_call_target="tpu_custom_call" | custom-call | tf_op jit(solution)/shard_map/finish/pallas_call | solution.py:543
